TPU v7x, 128 devices: a whole 4x4x4 slice. The times are simulated.
128 devices in a mesh: segment: 8 (over z, x_hi), replica: 16 (over x_lo, y, core).
Axes of the slice: x: 4 (x_hi: 2, x_lo: 2; x = x_hi * 2 + x_lo), y: 4, z: 4, core: 2. Of those that a mesh axis runs over, the one named last changes fastest.
Arguments:
- clips: bfloat16 [32, 4, 24, 16, 128], P('replica'), may hold values from -6 to 6
- offsets: int32 [32, 2], P('replica'), may hold values from 0 to 8
- weights: bfloat16 [8, 3456, 128], P('segment'), may hold values from -5 to 5
- moment: float32 [8, 3456, 128], P('segment', 'replica'), may hold values from -6 to 6
- second: float32 [8, 3456, 128], P('segment', 'replica'), may hold values from 0.25 to 4
- stale_grads: float32 [8, 3456, 128], P('segment', 'replica'), may hold values from -6 to 6
- cotangent: bfloat16 [32, 4, 16, 8, 128], P('replica'), may hold values from -6 to 6
Outputs:
- grads: float32 [8, 3456, 128], P('segment', 'replica')
- new_moment: float32 [8, 3456, 128], P('segment', 'replica')
- new_second: float32 [8, 3456, 128], P('segment', 'replica')
- new_weights: bfloat16 [8, 3456, 128], P('segment')
Inputs may be any that keep to these rules, and one draw needn't show every extreme that they name: `offsets`: each offset lets the tile lie inside its clip.
All inputs are finite; a program needn't handle non-finite values.
Results may differ from a plain program's by a relative error of at most 0.03.
Values may be sent and summed in bfloat16 or wider, within the bound.
A program may use at most 64 MiB of HBM per device.

v0:
```python
import math

import jax
import jax.numpy as jnp
from jax import lax
from jax.sharding import PartitionSpec as P

beta_one = 0.9
beta_two = 0.95
learn_rate = 0.05
adam_eps = 1e-08


def copy_for_each(shard, axis):
    count = lax.axis_size(axis)
    return lax.all_to_all(
        jnp.broadcast_to(shard[None], (count, *shard.shape)), axis, 0, 0, tiled=True
    )


def in_order(pieces, dim):
    pieces = jnp.moveaxis(pieces, 0, dim)
    shape = pieces.shape
    return pieces.reshape(*shape[:dim], shape[dim] * shape[dim + 1], *shape[dim + 2 :])


def gathered_copies(shard, axis, dim):
    pieces = copy_for_each(shard, axis)
    return in_order(pieces, dim)


def from_behind(value, axis, steps):
    count = lax.axis_size(axis)
    initial, last = (max(0, -steps), min(count, count - steps))
    return lax.ppermute(value, axis, [(source, source + steps) for source in range(initial, last)])


def split_up(shard, dim, count):
    before, after = (shard.shape[:dim], shard.shape[dim + 1 :])
    return jnp.moveaxis(shard.reshape(*before, count, -1, *after), dim, 0)


def sent_and_summed(shard, axis, dim):
    count = lax.axis_size(axis)
    pieces = lax.all_to_all(split_up(shard, dim, count), axis, 0, 0, tiled=True)
    return jnp.sum(pieces.astype(jnp.float32), axis=0)


def gather_taps(field):
    depth, height, width, chans = field.shape
    padded = jnp.pad(field, ((2, 0), (1, 1), (1, 1), (0, 0)))
    pieces = [
        padded[shift_t : shift_t + depth, shift_y : shift_y + height, shift_x : shift_x + width]
        for shift_t in range(3)
        for shift_y in range(3)
        for shift_x in range(3)
    ]
    return jnp.stack(pieces, axis=3).reshape(depth * height * width, 27 * chans)


def spread_taps(blocks, depth, height, width, chans):
    blocks = blocks.reshape(depth, height, width, 27, chans)
    total = jnp.zeros((depth + 2, height + 2, width + 2, chans), jnp.float32)
    index = 0
    for shift_t in range(3):
        for shift_y in range(3):
            for shift_x in range(3):
                total = total.at[
                    shift_t : shift_t + depth, shift_y : shift_y + height, shift_x : shift_x + width
                ].add(blocks[:, :, :, index])
                index = index + 1
    return total[2:, 1:-1, 1:-1]


def adam_rows(weights, moment, second, stale_grads):
    rows = moment.shape[1]
    start = lax.axis_index("replica") * rows
    local = lax.dynamic_slice_in_dim(weights[0], start, rows, 0).astype(jnp.float32)
    first_new = beta_one * moment[0] + (1.0 - beta_one) * stale_grads[0]
    second_new = beta_two * second[0] + (1.0 - beta_two) * stale_grads[0] * stale_grads[0]
    fresh = (local - learn_rate * first_new / (jnp.sqrt(second_new) + adam_eps)).astype(
        jnp.bfloat16
    )
    whole = gathered_copies(fresh, "replica", 0)
    return (first_new[None], second_new[None], whole[None])


def shards(clips, offsets, weights, moment, second, stale_grads, cotangent):
    micro, depth, clip_h, clip_w, chans = clips.shape
    height = cotangent.shape[2]
    width = cotangent.shape[3]
    cells = depth * height * width
    segments = lax.axis_size("segment")
    section = lax.axis_index("segment")
    matrix = weights[0]
    scale = 2.0 / math.sqrt(matrix.shape[0])
    anchor = jnp.zeros((), jnp.int32)
    ticks = micro + segments - 1
    kept_in = jnp.zeros((micro, depth, height, width, chans), jnp.bfloat16)
    kept_pre = jnp.zeros((micro, cells, chans), jnp.float32)

    def forward_tick(tick, carry):
        incoming, inputs_kept, pre_kept = carry
        slot = tick - section
        valid = (slot >= 0) & (slot < micro)
        place = jnp.clip(slot, 0, micro - 1)
        clip = lax.dynamic_index_in_dim(clips, place, 0, keepdims=False)
        offset = lax.dynamic_index_in_dim(offsets, place, 0, keepdims=False)
        crop = lax.dynamic_slice(
            clip, (anchor, offset[0], offset[1], anchor), (depth, height, width, chans)
        )
        field = jnp.where(section == 0, crop, incoming)
        patches = gather_taps(field)
        pre = jnp.dot(patches, matrix, preferred_element_type=jnp.float32) * scale
        old_in = lax.dynamic_index_in_dim(inputs_kept, place, 0, keepdims=False)
        inputs_kept = lax.dynamic_update_index_in_dim(
            inputs_kept, jnp.where(valid, field, old_in), place, 0
        )
        old_pre = lax.dynamic_index_in_dim(pre_kept, place, 0, keepdims=False)
        pre_kept = lax.dynamic_update_index_in_dim(
            pre_kept, jnp.where(valid, pre, old_pre), place, 0
        )
        output = jax.nn.silu(pre).astype(jnp.bfloat16).reshape(depth, height, width, chans)
        arriving = from_behind(output, "segment", 1)
        return (arriving, inputs_kept, pre_kept)

    empty_field = jnp.zeros((depth, height, width, chans), jnp.bfloat16)
    _, kept_in, kept_pre = lax.fori_loop(0, ticks, forward_tick, (empty_field, kept_in, kept_pre))

    def backward_tick(tick, carry):
        incoming, total = carry
        slot = tick - (segments - 1 - section)
        valid = (slot >= 0) & (slot < micro)
        place = jnp.clip(slot, 0, micro - 1)
        given = lax.dynamic_index_in_dim(cotangent, place, 0, keepdims=False)
        upstream = jnp.where(section == segments - 1, given, incoming).reshape(cells, chans)
        field = lax.dynamic_index_in_dim(kept_in, place, 0, keepdims=False)
        patches = gather_taps(field)
        pre = lax.dynamic_index_in_dim(kept_pre, place, 0, keepdims=False)
        sigma = jax.nn.sigmoid(pre)
        delta = (upstream.astype(jnp.float32) * sigma * (1.0 + pre * (1.0 - sigma))).astype(
            jnp.bfloat16
        )
        delta = jnp.where(valid, delta, jnp.zeros_like(delta))
        total = (
            total
            + lax.dot_general(
                patches, delta, (((0,), (0,)), ((), ())), preferred_element_type=jnp.float32
            )
            * scale
        )
        back = lax.dot_general(
            delta, matrix, (((1,), (1,)), ((), ())), preferred_element_type=jnp.float32
        )
        sent_back = (spread_taps(back, depth, height, width, chans) * scale).astype(jnp.bfloat16)
        arriving = from_behind(sent_back, "segment", -1)
        return (arriving, total)

    zero_total = jnp.zeros(matrix.shape, jnp.float32)
    _, total = lax.fori_loop(0, ticks, backward_tick, (empty_field, zero_total))
    tiles = micro * lax.axis_size("replica")
    terms = total * (4.0 / math.sqrt(tiles * cells))
    grads = sent_and_summed(terms.astype(jnp.bfloat16), "replica", 0)
    updated = adam_rows(weights, moment, second, stale_grads)
    first_new, second_new, whole = updated
    return (grads[None], first_new, second_new, whole)


def solution(mesh):
    placed = (
        P("replica", None, None, None, None),
        P("replica", None),
        P("segment", None, None),
        P("segment", "replica", None),
        P("segment", "replica", None),
        P("segment", "replica", None),
        P("replica", None, None, None, None),
    )
    return jax.shard_map(
        shards,
        mesh=mesh,
        in_specs=placed,
        out_specs=(
            P("segment", "replica", None),
            P("segment", "replica", None),
            P("segment", "replica", None),
            P("segment", None, None),
        ),
        check_vma=False,
    )
```

profile of v0, /device:TPU:1, one launch (start us, length us, event | category | flops | bytes accessed | tf_op | source)
XLA Modules:
  0.0 647.5 jit_solution(5472968268980505341)
XLA Ops:
  0.7 1.9 fusion.143
  3.6 6.9 %all-to-all-start.1 = ((bf16[16,216,128]{2,1,0:T(8,128)(2,1)}), bf16[16,216,128]{2,1,0:T(8,128)(2,1)}, u32[]{:S(2)}, u32[]{:S(2)}) async-start(bf16[16,216,128]{2,1,0:T(8,128)(2,1)} %broadcast_in_dim.55), calls=%async_computation.1 | async-start | bytes 1769472 | tf_op jit(solution)/shard_map/all_to_all | solution.py:16
  11.5 141.0 %while.66 = (s32[]{:T(128)}, bf16[4,16,8,128]{3,2,1,0:T(8,128)(2,1)S(1)}, bf16[2,4,16,8,128]{4,3,2,1,0:T(8,128)(2,1)S(1)}, f32[2,512,128]{2,1,0:T(8,128)}, pred[...) while((s32[]{:T(128)}, ...), condition=%wide.region_1.2_spmd, body=%wide.region_0.1_spmd.sunk | while | flops 453574656 | bytes 14647717 | solution.py:128
  19.4 4.4 collective-permute-start
  34.4 5.6 collective-permute-start
  49.8 5.3 collective-permute-start
  64.9 5.6 collective-permute-start
  80.3 6.2 collective-permute-start
  96.4 6.2 collective-permute-start
  112.4 6.2 collective-permute-start
  128.4 6.2 collective-permute-start
  144.4 6.2 collective-permute-start
  152.6 451.8 %while.67 = (s32[]{:T(128)}, bf16[4,16,8,128]{3,2,1,0:T(8,128)(2,1)S(1)}, f32[3456,128]{1,0:T(8,128)S(1)}, s32[]{:T(128)}, pred[]{:T(512)}, /*index=5*/bf16[2,4,...) while((s32[]{:T(128)}, ...), condition=%wide.region_3.4_spmd.clone, body=%wide.region_2.3_spmd.clone.sunk | while | flops 909918208 | bytes 91353544 | solution.py:160
  156.0 2.8 copy-done
  163.6 3.0 fusion.280
  166.5 2.3 scatter-add.212
  197.3 1.7 fusion.329
  199.0 4.1 collective-permute-done.1
  206.5 2.8 copy-done
  214.1 3.0 fusion.280
  217.1 2.3 scatter-add.212
  245.1 1.3 collective-permute-start.1
  247.8 1.7 fusion.329
  249.6 4.1 collective-permute-done.1
  257.0 2.8 copy-done
  264.6 3.0 fusion.280
  267.6 2.3 scatter-add.212
  298.4 1.7 fusion.329
  300.1 3.7 collective-permute-done.1
  307.1 2.8 copy-done
  314.7 3.0 fusion.280
  317.7 2.3 scatter-add.212
  345.7 1.3 collective-permute-start.1
  348.5 1.7 fusion.329
  350.2 3.7 collective-permute-done.1
  357.2 2.8 copy-done
  364.8 3.0 fusion.280
  367.8 2.3 scatter-add.212
  398.6 1.7 fusion.329
  400.3 3.7 collective-permute-done.1
  407.3 2.8 copy-done
  414.9 3.0 fusion.280
  417.9 2.3 scatter-add.212
  448.7 1.7 fusion.329
  450.4 3.7 collective-permute-done.1
  457.4 2.8 copy-done
  465.0 3.0 fusion.280
  468.0 2.3 scatter-add.212
  498.7 1.7 fusion.329
  500.5 3.7 collective-permute-done.1
  507.5 2.8 copy-done
  515.1 3.0 fusion.280
  518.1 2.3 scatter-add.212
  546.1 1.3 collective-permute-start.1
  548.8 1.7 fusion.329
  550.6 3.7 collective-permute-done.1
  557.6 2.8 copy-done
  565.2 3.0 fusion.280
  568.2 2.3 scatter-add.212
  598.9 1.7 fusion.329
  600.7 3.7 collective-permute-done.1
  605.4 25.4 %all-to-all-start = ((bf16[16,216,128]{2,1,0:T(8,128)(2,1)}), bf16[16,216,128]{2,1,0:T(8,128)(2,1)S(1)}, u32[]{:S(2)}, u32[]{:S(2)}) async-start(bf16[16,216,128]{2,1,0:T(8,128)(2,1)} %bitcast.755), calls=%async_computation | async-start | bytes 1769472 | tf_op jit(solution)/shard_map/all_to_all | solution.py:45
  630.7 13.9 %all-to-all-done = bf16[16,216,128]{2,1,0:T(8,128)(2,1)S(1)} async-done(((bf16[16,216,128]{2,1,0:T(8,128)(2,1)}), bf16[16,216,128]{2,1,0:T(8,128)(2,1)S(1)}, u32[]{:S(2)}, u32[]{:S(2)}) %all-to-all-start) | async-done | bytes 884768 | tf_op jit(solution)/shard_map/all_to_all | solution.py:45
  645.4 2.1 copy.244
  (1081 shorter events, 380.3 us)
Async XLA Ops:
  0.6 10.8 %copy-start.1 = (bf16[1,3456,128]{2,1,0:T(8,128)(2,1)S(1)}, bf16[1,3456,128]{2,1,0:T(8,128)(2,1)}, u32[]{:S(2)}) copy-start(bf16[1,3456,128]{2,1,0:T(8,128)(2,1)} %param.67) | copy-start | bytes 2654212
  0.6 10.8 %copy-start.4 = (s32[2,2]{1,0:T(2,128)S(1)}, s32[2,2]{1,0:T(2,128)}, u32[]{:S(2)}) copy-start(s32[2,2]{1,0:T(2,128)} %param.66) | copy-start | bytes 52
  3.6 601.7 %all-to-all-start.1 = ((bf16[16,216,128]{2,1,0:T(8,128)(2,1)}), bf16[16,216,128]{2,1,0:T(8,128)(2,1)}, u32[]{:S(2)}, u32[]{:S(2)}) async-start(bf16[16,216,128]{2,1,0:T(8,128)(2,1)} %broadcast_in_dim.55), calls=%async_computation.1 | async-start | bytes 1769472 | tf_op jit(solution)/shard_map/all_to_all | solution.py:16
  19.4 7.0 %collective-permute-start = (bf16[4,16,8,128]{3,2,1,0:T(8,128)(2,1)S(1)}, bf16[4,16,8,128]{3,2,1,0:T(8,128)(2,1)S(1)}, u32[]{:S(2)}, u32[]{:S(2)}) collective-permute-start(bf16[4,16,8,128]{3,2,1,0:T(8,128)(2,1)S(1)} %bitcast.758), channel_id=1, source_target_pairs={{0,16},{16,32},{32,48},{48,64},{64,80},{80,96},{96,112},{1,17},{17... | collective-permute-start | bytes 393224 | tf_op jit(solution)/shard_map/while/body/eval_jaxpr/ppermute | solution.py:35
  34.4 7.5 %collective-permute-start = (bf16[4,16,8,128]{3,2,1,0:T(8,128)(2,1)S(1)}, bf16[4,16,8,128]{3,2,1,0:T(8,128)(2,1)S(1)}, u32[]{:S(2)}, u32[]{:S(2)}) collective-permute-start(bf16[4,16,8,128]{3,2,1,0:T(8,128)(2,1)S(1)} %bitcast.758), channel_id=1, source_target_pairs={{0,16},{16,32},{32,48},{48,64},{64,80},{80,96},{96,112},{1,17},{17... | collective-permute-start | bytes 393224 | tf_op jit(solution)/shard_map/while/body/eval_jaxpr/ppermute | solution.py:35
  49.8 7.2 %collective-permute-start = (bf16[4,16,8,128]{3,2,1,0:T(8,128)(2,1)S(1)}, bf16[4,16,8,128]{3,2,1,0:T(8,128)(2,1)S(1)}, u32[]{:S(2)}, u32[]{:S(2)}) collective-permute-start(bf16[4,16,8,128]{3,2,1,0:T(8,128)(2,1)S(1)} %bitcast.758), channel_id=1, source_target_pairs={{0,16},{16,32},{32,48},{48,64},{64,80},{80,96},{96,112},{1,17},{17... | collective-permute-start | bytes 393224 | tf_op jit(solution)/shard_map/while/body/eval_jaxpr/ppermute | solution.py:35
  64.9 7.5 %collective-permute-start = (bf16[4,16,8,128]{3,2,1,0:T(8,128)(2,1)S(1)}, bf16[4,16,8,128]{3,2,1,0:T(8,128)(2,1)S(1)}, u32[]{:S(2)}, u32[]{:S(2)}) collective-permute-start(bf16[4,16,8,128]{3,2,1,0:T(8,128)(2,1)S(1)} %bitcast.758), channel_id=1, source_target_pairs={{0,16},{16,32},{32,48},{48,64},{64,80},{80,96},{96,112},{1,17},{17... | collective-permute-start | bytes 393224 | tf_op jit(solution)/shard_map/while/body/eval_jaxpr/ppermute | solution.py:35
  80.3 8.1 %collective-permute-start = (bf16[4,16,8,128]{3,2,1,0:T(8,128)(2,1)S(1)}, bf16[4,16,8,128]{3,2,1,0:T(8,128)(2,1)S(1)}, u32[]{:S(2)}, u32[]{:S(2)}) collective-permute-start(bf16[4,16,8,128]{3,2,1,0:T(8,128)(2,1)S(1)} %bitcast.758), channel_id=1, source_target_pairs={{0,16},{16,32},{32,48},{48,64},{64,80},{80,96},{96,112},{1,17},{17... | collective-permute-start | bytes 393224 | tf_op jit(solution)/shard_map/while/body/eval_jaxpr/ppermute | solution.py:35
  96.4 8.1 %collective-permute-start = (bf16[4,16,8,128]{3,2,1,0:T(8,128)(2,1)S(1)}, bf16[4,16,8,128]{3,2,1,0:T(8,128)(2,1)S(1)}, u32[]{:S(2)}, u32[]{:S(2)}) collective-permute-start(bf16[4,16,8,128]{3,2,1,0:T(8,128)(2,1)S(1)} %bitcast.758), channel_id=1, source_target_pairs={{0,16},{16,32},{32,48},{48,64},{64,80},{80,96},{96,112},{1,17},{17... | collective-permute-start | bytes 393224 | tf_op jit(solution)/shard_map/while/body/eval_jaxpr/ppermute | solution.py:35
  112.4 8.1 %collective-permute-start = (bf16[4,16,8,128]{3,2,1,0:T(8,128)(2,1)S(1)}, bf16[4,16,8,128]{3,2,1,0:T(8,128)(2,1)S(1)}, u32[]{:S(2)}, u32[]{:S(2)}) collective-permute-start(bf16[4,16,8,128]{3,2,1,0:T(8,128)(2,1)S(1)} %bitcast.758), channel_id=1, source_target_pairs={{0,16},{16,32},{32,48},{48,64},{64,80},{80,96},{96,112},{1,17},{17... | collective-permute-start | bytes 393224 | tf_op jit(solution)/shard_map/while/body/eval_jaxpr/ppermute | solution.py:35
  128.4 8.1 %collective-permute-start = (bf16[4,16,8,128]{3,2,1,0:T(8,128)(2,1)S(1)}, bf16[4,16,8,128]{3,2,1,0:T(8,128)(2,1)S(1)}, u32[]{:S(2)}, u32[]{:S(2)}) collective-permute-start(bf16[4,16,8,128]{3,2,1,0:T(8,128)(2,1)S(1)} %bitcast.758), channel_id=1, source_target_pairs={{0,16},{16,32},{32,48},{48,64},{64,80},{80,96},{96,112},{1,17},{17... | collective-permute-start | bytes 393224 | tf_op jit(solution)/shard_map/while/body/eval_jaxpr/ppermute | solution.py:35
  144.4 8.1 %collective-permute-start = (bf16[4,16,8,128]{3,2,1,0:T(8,128)(2,1)S(1)}, bf16[4,16,8,128]{3,2,1,0:T(8,128)(2,1)S(1)}, u32[]{:S(2)}, u32[]{:S(2)}) collective-permute-start(bf16[4,16,8,128]{3,2,1,0:T(8,128)(2,1)S(1)} %bitcast.758), channel_id=1, source_target_pairs={{0,16},{16,32},{32,48},{48,64},{64,80},{80,96},{96,112},{1,17},{17... | collective-permute-start | bytes 393224 | tf_op jit(solution)/shard_map/while/body/eval_jaxpr/ppermute | solution.py:35
  152.6 3.3 copy-start.2
  155.9 2.9 copy-start
  194.6 8.5 %collective-permute-start.1 = (bf16[4,16,8,128]{3,2,1,0:T(8,128)(2,1)S(1)}, bf16[4,16,8,128]{3,2,1,0:T(8,128)(2,1)S(1)}, u32[]{:S(2)}, u32[]{:S(2)}) collective-permute-start(bf16[4,16,8,128]{3,2,1,0:T(8,128)(2,1)S(1)} %fusion.302), channel_id=1, source_target_pairs={{16,0},{32,16},{48,32},{64,48},{80,64},{96,80},{112,96},{17,1},{33... | collective-permute-start | bytes 393224 | tf_op jit(solution)/shard_map/while/body/eval_jaxpr/ppermute | solution.py:35
  197.3 5.8 copy-start.3
  203.2 3.3 copy-start.2
  206.4 2.9 copy-start
  245.1 8.5 %collective-permute-start.1 = (bf16[4,16,8,128]{3,2,1,0:T(8,128)(2,1)S(1)}, bf16[4,16,8,128]{3,2,1,0:T(8,128)(2,1)S(1)}, u32[]{:S(2)}, u32[]{:S(2)}) collective-permute-start(bf16[4,16,8,128]{3,2,1,0:T(8,128)(2,1)S(1)} %fusion.302), channel_id=1, source_target_pairs={{16,0},{32,16},{48,32},{64,48},{80,64},{96,80},{112,96},{17,1},{33... | collective-permute-start | bytes 393224 | tf_op jit(solution)/shard_map/while/body/eval_jaxpr/ppermute | solution.py:35
  247.8 5.8 copy-start.3
  253.7 3.3 copy-start.2
  257.0 2.9 copy-start
  295.7 8.1 %collective-permute-start.1 = (bf16[4,16,8,128]{3,2,1,0:T(8,128)(2,1)S(1)}, bf16[4,16,8,128]{3,2,1,0:T(8,128)(2,1)S(1)}, u32[]{:S(2)}, u32[]{:S(2)}) collective-permute-start(bf16[4,16,8,128]{3,2,1,0:T(8,128)(2,1)S(1)} %fusion.302), channel_id=1, source_target_pairs={{16,0},{32,16},{48,32},{64,48},{80,64},{96,80},{112,96},{17,1},{33... | collective-permute-start | bytes 393224 | tf_op jit(solution)/shard_map/while/body/eval_jaxpr/ppermute | solution.py:35
  298.3 5.4 copy-start.3
  303.8 3.3 copy-start.2
  307.0 2.9 copy-start
  345.7 8.1 %collective-permute-start.1 = (bf16[4,16,8,128]{3,2,1,0:T(8,128)(2,1)S(1)}, bf16[4,16,8,128]{3,2,1,0:T(8,128)(2,1)S(1)}, u32[]{:S(2)}, u32[]{:S(2)}) collective-permute-start(bf16[4,16,8,128]{3,2,1,0:T(8,128)(2,1)S(1)} %fusion.302), channel_id=1, source_target_pairs={{16,0},{32,16},{48,32},{64,48},{80,64},{96,80},{112,96},{17,1},{33... | collective-permute-start | bytes 393224 | tf_op jit(solution)/shard_map/while/body/eval_jaxpr/ppermute | solution.py:35
  348.4 5.4 copy-start.3
  353.9 3.3 copy-start.2
  357.1 2.9 copy-start
  395.8 8.1 %collective-permute-start.1 = (bf16[4,16,8,128]{3,2,1,0:T(8,128)(2,1)S(1)}, bf16[4,16,8,128]{3,2,1,0:T(8,128)(2,1)S(1)}, u32[]{:S(2)}, u32[]{:S(2)}) collective-permute-start(bf16[4,16,8,128]{3,2,1,0:T(8,128)(2,1)S(1)} %fusion.302), channel_id=1, source_target_pairs={{16,0},{32,16},{48,32},{64,48},{80,64},{96,80},{112,96},{17,1},{33... | collective-permute-start | bytes 393224 | tf_op jit(solution)/shard_map/while/body/eval_jaxpr/ppermute | solution.py:35
  398.5 5.4 copy-start.3
  404.0 3.3 copy-start.2
  407.2 2.9 copy-start
  445.9 8.1 %collective-permute-start.1 = (bf16[4,16,8,128]{3,2,1,0:T(8,128)(2,1)S(1)}, bf16[4,16,8,128]{3,2,1,0:T(8,128)(2,1)S(1)}, u32[]{:S(2)}, u32[]{:S(2)}) collective-permute-start(bf16[4,16,8,128]{3,2,1,0:T(8,128)(2,1)S(1)} %fusion.302), channel_id=1, source_target_pairs={{16,0},{32,16},{48,32},{64,48},{80,64},{96,80},{112,96},{17,1},{33... | collective-permute-start | bytes 393224 | tf_op jit(solution)/shard_map/while/body/eval_jaxpr/ppermute | solution.py:35
  448.6 5.4 copy-start.3
  454.1 3.3 copy-start.2
  457.3 2.9 copy-start
  496.0 8.1 %collective-permute-start.1 = (bf16[4,16,8,128]{3,2,1,0:T(8,128)(2,1)S(1)}, bf16[4,16,8,128]{3,2,1,0:T(8,128)(2,1)S(1)}, u32[]{:S(2)}, u32[]{:S(2)}) collective-permute-start(bf16[4,16,8,128]{3,2,1,0:T(8,128)(2,1)S(1)} %fusion.302), channel_id=1, source_target_pairs={{16,0},{32,16},{48,32},{64,48},{80,64},{96,80},{112,96},{17,1},{33... | collective-permute-start | bytes 393224 | tf_op jit(solution)/shard_map/while/body/eval_jaxpr/ppermute | solution.py:35
  498.7 5.4 copy-start.3
  504.2 3.3 copy-start.2
  507.4 2.9 copy-start
  546.1 8.1 %collective-permute-start.1 = (bf16[4,16,8,128]{3,2,1,0:T(8,128)(2,1)S(1)}, bf16[4,16,8,128]{3,2,1,0:T(8,128)(2,1)S(1)}, u32[]{:S(2)}, u32[]{:S(2)}) collective-permute-start(bf16[4,16,8,128]{3,2,1,0:T(8,128)(2,1)S(1)} %fusion.302), channel_id=1, source_target_pairs={{16,0},{32,16},{48,32},{64,48},{80,64},{96,80},{112,96},{17,1},{33... | collective-permute-start | bytes 393224 | tf_op jit(solution)/shard_map/while/body/eval_jaxpr/ppermute | solution.py:35
  548.8 5.4 copy-start.3
  554.2 3.3 copy-start.2
  557.5 2.9 copy-start
  596.2 8.1 %collective-permute-start.1 = (bf16[4,16,8,128]{3,2,1,0:T(8,128)(2,1)S(1)}, bf16[4,16,8,128]{3,2,1,0:T(8,128)(2,1)S(1)}, u32[]{:S(2)}, u32[]{:S(2)}) collective-permute-start(bf16[4,16,8,128]{3,2,1,0:T(8,128)(2,1)S(1)} %fusion.302), channel_id=1, source_target_pairs={{16,0},{32,16},{48,32},{64,48},{80,64},{96,80},{112,96},{17,1},{33... | collective-permute-start | bytes 393224 | tf_op jit(solution)/shard_map/while/body/eval_jaxpr/ppermute | solution.py:35
  598.9 5.4 copy-start.3
  605.4 39.3 %all-to-all-start = ((bf16[16,216,128]{2,1,0:T(8,128)(2,1)}), bf16[16,216,128]{2,1,0:T(8,128)(2,1)S(1)}, u32[]{:S(2)}, u32[]{:S(2)}) async-start(bf16[16,216,128]{2,1,0:T(8,128)(2,1)} %bitcast.755), calls=%async_computation | async-start | bytes 1769472 | tf_op jit(solution)/shard_map/all_to_all | solution.py:45
where the time goes:
time: 659 us; the launch traced here: 648 us
  other arithmetic  272 us (41%)
  local copies, waits for them, and re-layouts  154 us (23%)
  starting transfers between devices  95.7 us (15%)
  waiting for transfers between devices  50.4 us (8%)
  loops' own time  38.9 us (6%)
  matrix products  35.1 us (5%)
    add x162, other arithmetic, spread_taps(): total = total.at[shift_t:shift_t + depth, shift_y:shift_y + height, shift...  170 us
    scatter-add x72, other arithmetic, spread_taps(): total = total.at[shift_t:shift_t + depth, shift_y:shift_y + height, shift...  72.6 us
    scatter-add x171, local copies, waits for them, and re-layouts, spread_taps(): total = total.at[shift_t:shift_t + depth, shift_y:shift_y + height, shift...  71.7 us
    ppermute x18, starting transfers between devices, from_behind(): lax.ppermute(value, axis, [(source, source + steps) for source in range(i...  63.4 us
    while x522, local copies, waits for them, and re-layouts  46.4 us
    ppermute x18, waiting for transfers between devices, from_behind(): lax.ppermute(value, axis, [(source, source + steps) for source in range(i...  36.5 us
    another operation x1, loops' own time, shards(): lax.fori_loop(0, ticks, forward_tick, (empty_field, kept_in, kept_pre))  34.9 us
    all_to_all x1, starting transfers between devices, sent_and_summed(): pieces = lax.all_to_all(split_up(shard, dim, count), axis, 0, 0, tiled=True)  25.4 us
  transfers between devices with their start and end apart: 20, of which 19 were waited for; matrix products, arithmetic and copies ran while one was open for 67% of the time, Pallas kernels for 0%

commit v1 on v0

v1 whole, which is shorter than its diff:
```python
import math

import jax
import jax.numpy as jnp
from jax import lax
from jax.experimental import pallas as pl
from jax.experimental.pallas import tpu as pltpu
from jax.sharding import PartitionSpec as P

beta_one = 0.9
beta_two = 0.95
learn_rate = 0.05
adam_eps = 1e-08

F32 = jnp.float32
BF16 = jnp.bfloat16
FRAMES, HEIGHT, WIDTH, CHAN = 4, 16, 8, 128
PLANE = HEIGHT * WIDTH
CELLS = FRAMES * PLANE
SECTIONS = 8
TAPS = 27
ROWS = TAPS * CHAN
SCALE = 2.0 / math.sqrt(ROWS)
GRAD_SCALE = SCALE * 4.0 / math.sqrt(32 * CELLS)


def dot(a, b):
    return jnp.dot(a, b, preferred_element_type=F32)


def store_shifted(store, value):
    row = lax.broadcasted_iota(jnp.int32, (CELLS, CHAN), 0) % HEIGHT
    zero = jnp.zeros_like(value)
    for b in range(3):
        if b == 0:
            moved = jnp.where(row == 0, zero, pltpu.roll(value, 1, 0))
        elif b == 1:
            moved = value
        else:
            moved = jnp.where(row == HEIGHT - 1, zero, pltpu.roll(value, CELLS - 1, 0))
        store(b, moved.astype(BF16).reshape(FRAMES, WIDTH, HEIGHT, CHAN))


def forward_section(s, w, taps, slope, last):
    total = None
    pieces = []
    for a in range(3):
        frames = 2 + a
        first = FRAMES - frames
        lhs = jnp.concatenate(
            [
                taps[s, a + first : a + FRAMES, c : c + WIDTH].reshape(frames * PLANE, 3 * CHAN)
                for c in range(3)
            ],
            axis=1,
        )
        rhs = jnp.concatenate(
            [w[s, (a * 3 + b) * 3 + c] for c in range(3) for b in range(3)], axis=0
        )
        pieces.append(dot(lhs, rhs))
    total = pieces[2]
    total = jnp.concatenate(
        [
            total[:PLANE],
            total[PLANE : 2 * PLANE] + pieces[1][:PLANE],
            total[2 * PLANE :] + pieces[1][PLANE:] + pieces[0],
        ],
        axis=0,
    )
    pre = total * SCALE
    sigma = jax.nn.sigmoid(pre)
    slope[s] = sigma * (1.0 + pre * (1.0 - sigma))

    @pl.when(s < last)
    def _():
        def store(b, moved):
            taps[s + 1, 2:, 1 : 1 + WIDTH, :, b * CHAN : (b + 1) * CHAN] = moved

        store_shifted(store, pre * sigma)


def shifted_delta(s, upstream, slope, back):
    delta = upstream[...] * slope[s]

    def store(b, moved):
        back[:FRAMES, 1 : 1 + WIDTH, :, b * CHAN : (b + 1) * CHAN] = moved

    store_shifted(store, delta)


def weight_grad(s, taps, back, put):
    field = taps[s, 2:, 1 : 1 + WIDTH, :, CHAN : 2 * CHAN].reshape(CELLS, CHAN)
    turned = field.astype(F32).T.astype(BF16)
    for a in range(3):
        frames = 2 + a
        lhs = turned[:, : frames * PLANE]
        for c in range(3):
            rhs = back[2 - a : 2 - a + frames, 2 - c : 2 - c + WIDTH].reshape(
                frames * PLANE, 3 * CHAN
            )
            out = dot(lhs, rhs) * GRAD_SCALE
            for b in range(3):
                put((a * 3 + b) * 3 + c, out[:, (2 - b) * CHAN : (3 - b) * CHAN])


def input_grad(s, w, back, upstream):
    pieces = []
    for a in range(3):
        frames = 2 + a
        lhs = jnp.concatenate(
            [
                back[2 - a : 2 - a + frames, 2 - c : 2 - c + WIDTH].reshape(
                    frames * PLANE, 3 * CHAN
                )
                for c in range(3)
            ],
            axis=1,
        )
        rhs = jnp.concatenate(
            [w[s, (a * 3 + 2 - b) * 3 + c] for c in range(3) for b in range(3)], axis=1
        )
        pieces.append(
            lax.dot_general(lhs, rhs, (((1,), (1,)), ((), ())), preferred_element_type=F32)
        )
    total = pieces[2]
    total = jnp.concatenate(
        [
            total[: 2 * PLANE] + pieces[1][: 2 * PLANE] + pieces[0],
            total[2 * PLANE : 3 * PLANE] + pieces[1][2 * PLANE :],
            total[3 * PLANE :],
        ],
        axis=0,
    )
    upstream[...] = total * SCALE


def crop(clip, offset_y, offset_x, taps):
    row = lax.broadcasted_iota(jnp.int32, (PLANE, clip.shape[-2]), 0)
    col = lax.broadcasted_iota(jnp.int32, (PLANE, clip.shape[-2]), 1)
    clip_w = 16
    want = (row % HEIGHT + offset_y) * clip_w + row // HEIGHT + offset_x
    pick = jnp.where(want == col, 1.0, 0.0).astype(BF16)
    field = jnp.concatenate([dot(pick, clip[t]) for t in range(FRAMES)], axis=0)

    def store(b, moved):
        taps[0, 2:, 1 : 1 + WIDTH, :, b * CHAN : (b + 1) * CHAN] = moved

    store_shifted(store, field)


def reorder(cotangent, upstream):
    row = lax.broadcasted_iota(jnp.int32, (PLANE, PLANE), 0)
    col = lax.broadcasted_iota(jnp.int32, (PLANE, PLANE), 1)
    pick = jnp.where(row % HEIGHT * WIDTH + row // HEIGHT == col, 1.0, 0.0).astype(BF16)
    for t in range(FRAMES):
        upstream[t * PLANE : (t + 1) * PLANE] = dot(pick, cotangent[t])


def clear_edges(taps, back):
    def wipe(s, _):
        taps[s, :2] = jnp.zeros((2, WIDTH + 2, HEIGHT, 3 * CHAN), BF16)
        taps[s, 2:, 0] = jnp.zeros((FRAMES, HEIGHT, 3 * CHAN), BF16)
        taps[s, 2:, WIDTH + 1] = jnp.zeros((FRAMES, HEIGHT, 3 * CHAN), BF16)
        return 0

    lax.fori_loop(0, SECTIONS, wipe, 0)
    back[FRAMES:] = jnp.zeros((2, WIDTH + 2, HEIGHT, 3 * CHAN), BF16)
    back[:FRAMES, 0] = jnp.zeros((FRAMES, HEIGHT, 3 * CHAN), BF16)
    back[:FRAMES, WIDTH + 1] = jnp.zeros((FRAMES, HEIGHT, 3 * CHAN), BF16)


def window_kernel(offsets, clips, w, cotangent, out, taps, back, slope, upstream):
    segment = lax.axis_index("segment")
    depth = segment // 2
    mine = segment % 2
    clear_edges(taps, back)
    crop(clips.at[mine], offsets[mine, 0], offsets[mine, 1], taps)
    reorder(cotangent.at[mine], upstream)

    def forward(s, _):
        forward_section(s, w, taps, slope, SECTIONS - 1)
        return 0

    lax.fori_loop(0, SECTIONS, forward, 0)

    def backward(i, _):
        s = SECTIONS - 1 - i
        shifted_delta(s, upstream, slope, back)

        @pl.when(s // 2 == depth)
        def _():
            def put(tap, block):
                out[s % 2, tap] = block.astype(BF16)

            weight_grad(s, taps, back, put)

        @pl.when(s > 0)
        def _():
            input_grad(s, w, back, upstream)

        return 0

    lax.fori_loop(0, SECTIONS, backward, 0)


def window(offsets, clips, w, cotangent):
    vmem = pl.BlockSpec(memory_space=pltpu.VMEM)
    return pl.pallas_call(
        window_kernel,
        out_shape=jax.ShapeDtypeStruct((2, TAPS, CHAN, CHAN), BF16),
        in_specs=[pl.BlockSpec(memory_space=pltpu.SMEM), vmem, vmem, vmem],
        out_specs=vmem,
        scratch_shapes=[
            pltpu.VMEM((SECTIONS, FRAMES + 2, WIDTH + 2, HEIGHT, 3 * CHAN), BF16),
            pltpu.VMEM((FRAMES + 2, WIDTH + 2, HEIGHT, 3 * CHAN), BF16),
            pltpu.VMEM((SECTIONS, CELLS, CHAN), F32),
            pltpu.VMEM((CELLS, CHAN), F32),
        ],
        compiler_params=pltpu.CompilerParams(vmem_limit_bytes=56 << 20),
    )(offsets, clips, w, cotangent)


def adam_rows(weights, moment, second, stale_grads):
    rows = moment.shape[1]
    start = lax.axis_index("replica") * rows
    local = lax.dynamic_slice_in_dim(weights[0], start, rows, 0).astype(F32)
    first_new = beta_one * moment[0] + (1.0 - beta_one) * stale_grads[0]
    second_new = beta_two * second[0] + (1.0 - beta_two) * stale_grads[0] * stale_grads[0]
    fresh = (local - learn_rate * first_new / (jnp.sqrt(second_new) + adam_eps)).astype(BF16)
    whole = lax.all_gather(fresh, "replica", axis=0, tiled=True)
    return (first_new[None], second_new[None], whole[None])


def shards(clips, offsets, weights, moment, second, stale_grads, cotangent):
    micro = clips.shape[0]
    mine = lax.axis_index("segment") % 2
    gathered = lax.all_gather(weights[0], "segment", axis=0)
    partial = window(
        offsets,
        clips.reshape(micro, FRAMES, -1, CHAN),
        gathered.reshape(SECTIONS, TAPS, CHAN, CHAN),
        cotangent.reshape(micro, FRAMES, PLANE, CHAN),
    )
    keep = lax.dynamic_index_in_dim(partial, mine, 0, keepdims=False)
    give = lax.dynamic_index_in_dim(partial, 1 - mine, 0, keepdims=False)
    taken = lax.ppermute(give, "segment", [(s, s ^ 1) for s in range(SECTIONS)])
    pair = (keep.astype(F32) + taken.astype(F32)).astype(BF16)
    count = lax.axis_size("replica")
    pieces = lax.all_to_all(pair.reshape(count, -1, CHAN), "replica", 0, 0, tiled=True)
    grads = jnp.sum(pieces.astype(F32), axis=0)
    first_new, second_new, whole = adam_rows(weights, moment, second, stale_grads)
    return (grads[None], first_new, second_new, whole)


def solution(mesh):
    placed = (
        P("replica", None, None, None, None),
        P("replica", None),
        P("segment", None, None),
        P("segment", "replica", None),
        P("segment", "replica", None),
        P("segment", "replica", None),
        P("replica", None, None, None, None),
    )
    return jax.shard_map(
        shards,
        mesh=mesh,
        in_specs=placed,
        out_specs=(
            P("segment", "replica", None),
            P("segment", "replica", None),
            P("segment", "replica", None),
            P("segment", None, None),
        ),
        check_vma=False,
    )
```

time: 659 us -> 198 us (0.30); the launches traced: 648 us -> 198 us
  other arithmetic: 272 us -> 3.61 us
  local copies, waits for them, and re-layouts: 154 us -> 2.28 us
  starting transfers between devices: 95.7 us -> 6.96 us
  waiting for transfers between devices: 50.4 us -> 122 us
  loops' own time: 38.9 us -> 0 us
  matrix products: 35.1 us -> 0 us
  blocking collectives: 0 us -> 28 us
  Pallas kernels: 0 us -> 21.2 us
  between operations: 0.69 us -> 14.1 us
    add x162 -> x1, other arithmetic: 170 us -> 0.72 us  [adam_rows(): beta_two * second[0] + (1.0 - beta_two) * stale_grads[0] * stale_grads[0]]
    all_gather x0 -> x1, waiting for transfers between devices: none -> 100 us  [shards(): gathered = lax.all_gather(weights[0], 'segment', axis=0)]
    scatter-add x72 -> x0, other arithmetic: 72.6 us -> none  [spread_taps(): total = total.at[shift_t:shift_t + depth, shift_y:shift_y + height, shift...]
    scatter-add x171 -> x0, local copies, waits for them, and re-layouts: 71.7 us -> none  [spread_taps(): total = total.at[shift_t:shift_t + depth, shift_y:shift_y + height, shift...]
    ppermute x18 -> x1, starting transfers between devices: 63.4 us -> 0.35 us  [shards(): taken = lax.ppermute(give, 'segment', [(s, s ^ 1) for s in range(SECTIONS)])]
    while x522 -> x0, local copies, waits for them, and re-layouts: 46.4 us -> none
    another operation x2 -> x0, loops' own time: 38.9 us -> none  [the longest x1 34.9 us: shards(): lax.fori_loop(0, ticks, forward_tick, (empty_field, kept_in, kept_pre))]
    dot_general x27 -> x0, matrix products: 35.1 us -> none  [the longest x9 15.4 us: backward_tick(): lax.dot_general(patches, delta, (((0,), (0,)), ((), ())), preferred_eleme...]
  transfers between devices with their start and end apart: 20 -> 3, of which waited for: 19 -> 2; matrix products, arithmetic and copies ran while one was open for 67% -> 1% of each run, Pallas kernels for 0% -> 0%
where the time goes in v1:
time: 198 us
  waiting for transfers between devices  122 us (62%)
  blocking collectives  28 us (14%)
  Pallas kernels  21.2 us (11%)
  between operations  14.1 us (7%)
  starting transfers between devices  6.96 us (4%)
  other arithmetic  3.61 us (2%)
  local copies, waits for them, and re-layouts  2.28 us (1%)
    all_gather x1, waiting for transfers between devices, shards(): gathered = lax.all_gather(weights[0], 'segment', axis=0)  100 us
    all_gather x1, blocking collectives, adam_rows(): whole = lax.all_gather(fresh, 'replica', axis=0, tiled=True)  28 us
    pallas_call x1, Pallas kernels, window(): pl.pallas_call(window_kernel, out_shape=jax.ShapeDtypeStruct((2, TAPS, CH...  21.2 us
    ppermute x1, waiting for transfers between devices, shards(): taken = lax.ppermute(give, 'segment', [(s, s ^ 1) for s in range(SECTIONS)])  21 us
    all_to_all x1, starting transfers between devices, shards(): lax.all_to_all(pair.reshape(count, -1, CHAN), 'replica', 0, 0, tiled=True)  6.57 us
  transfers between devices with their start and end apart: 3, of which 2 were waited for; matrix products, arithmetic and copies ran while one was open for 1% of the time, Pallas kernels for 0%

profile of v1, /device:TPU:1, one launch (start us, length us, event | category | flops | bytes accessed | tf_op | source)
XLA Modules:
  0.0 198.0 jit_solution(18240815180939914877)
XLA Ops:
  7.2 0.0 all-gather.2.cloned.1.call-start
  7.2 0.7 all-gather.2.cloned.1.call-update
  7.9 100.2 %all-gather.2.cloned.1.call-done = bf16[8,3456,128]{2,1,0:T(8,128)(2,1)} async-done(((bf16[1,3456,128]{2,1,0:T(8,128)(2,1)}), bf16[8,3456,128]{2,1,0:T(8,128)(2,1)}) %all-gather.2.cloned.1.call-update) | async-done | bytes 7077904 | tf_op jit(solution)/shard_map/all_gather | solution.py:237
  108.1 21.2 %shard_map.102 = bf16[2,27,128,128]{3,2,1,0:T(8,128)(2,1)} custom-call(s32[2,2]{1,0:T(2,128)} %offsets.1, bf16[2,4,384,128]{3,2,1,0:T(8,128)(2,1)} %bitcast.35, bf16[8,27,128,128]{3,2,1,0:T(8,128)(2,1)} %bitcast.33, bf16[2,4,128,128]{3,2,1,0:T(8,128)(2,1)} %bitcast.36), custom_call_target="tpu_custom_call" | custom-call | tf_op jit(solution)/shard_map/pallas_call | solution.py:208
  129.3 0.0 copy-start
  129.3 1.4 dynamic-slice_bitcast_fusion
  130.7 0.4 collective-permute-start
  131.0 21.0 %collective-permute-done = bf16[27,128,128]{2,1,0:T(8,128)(2,1)S(1)} collective-permute-done((bf16[27,128,128]{2,1,0:T(8,128)(2,1)S(1)}, bf16[27,128,128]{2,1,0:T(8,128)(2,1)S(1)}, u32[]{:S(2)}, u32[]{:S(2)}) %collective-permute-start) | collective-permute-done | bytes 884768 | tf_op jit(solution)/shard_map/ppermute | solution.py:246
  152.0 0.0 copy-done
  152.1 0.0 copy-start.1
  152.1 0.0 copy-start.2
  152.1 0.0 copy-start.3
  152.1 1.2 fusion
  153.3 6.6 %all-to-all-start = ((bf16[16,216,128]{2,1,0:T(8,128)(2,1)}), bf16[16,216,128]{2,1,0:T(8,128)(2,1)S(1)}, u32[]{:S(2)}, u32[]{:S(2)}) async-start(bf16[16,216,128]{2,1,0:T(8,128)(2,1)} %bitcast.5), calls=%async_computation | async-start | bytes 1769472 | tf_op jit(solution)/shard_map/all_to_all | solution.py:249
  159.8 0.0 copy-done.1
  159.9 0.0 copy-done.2
  159.9 0.0 copy-done.3
  159.9 0.9 fusion.9
  160.8 28.0 %all_gather.7 = bf16[3456,128]{1,0:T(8,128)(2,1)S(1)} all-gather(bf16[216,128]{1,0:T(8,128)(2,1)S(1)} %fusion.9), channel_id=1, replica_groups=mesh['segment'=8,'replica'=16] {'replica'}, dimensions={0}, use_global_device_ids=true | all-gather | bytes 940032 | tf_op jit(solution)/shard_map/all_gather | solution.py:230
  188.7 0.7 fusion.1
  189.5 0.0 all-to-all-done
  189.5 0.8 convert_reduce_fusion
  190.2 0.9 copy.12
Async XLA Ops:
  7.2 100.9 %all-gather.2.cloned.1.call-start = ((), (), s32[]{:S(2)}) async-start(), calls=%async_computation.1 | async-start | bytes 7962624 | tf_op jit(solution)/shard_map/all_gather | solution.py:237
  129.3 22.7 %copy-start = (bf16[2,27,128,128]{3,2,1,0:T(8,128)(2,1)S(1)}, bf16[2,27,128,128]{3,2,1,0:T(8,128)(2,1)}, u32[]{:S(2)}) copy-start(bf16[2,27,128,128]{3,2,1,0:T(8,128)(2,1)} %shard_map.102) | copy-start | bytes 5308420
  130.7 21.4 %collective-permute-start = (bf16[27,128,128]{2,1,0:T(8,128)(2,1)S(1)}, bf16[27,128,128]{2,1,0:T(8,128)(2,1)S(1)}, u32[]{:S(2)}, u32[]{:S(2)}) collective-permute-start(bf16[27,128,128]{2,1,0:T(8,128)(2,1)S(1)} %dynamic-slice_bitcast_fusion), channel_id=1, source_target_pairs={{0,16},{16,0},{32,48},{48,32},{64,80},{80,64},{96,112},{112,96},{1... | collective-permute-start | bytes 2654216 | tf_op jit(solution)/shard_map/ppermute | solution.py:246
  152.1 7.8 %copy-start.1 = (f32[1,216,128]{2,1,0:T(8,128)S(1)}, f32[1,216,128]{2,1,0:T(8,128)}, u32[]{:S(2)}) copy-start(f32[1,216,128]{2,1,0:T(8,128)} %param.12) | copy-start | bytes 331780
  152.1 7.8 %copy-start.2 = (f32[1,216,128]{2,1,0:T(8,128)S(1)}, f32[1,216,128]{2,1,0:T(8,128)}, u32[]{:S(2)}) copy-start(f32[1,216,128]{2,1,0:T(8,128)} %param.11) | copy-start | bytes 331780
  152.1 7.8 %copy-start.3 = (f32[1,216,128]{2,1,0:T(8,128)S(1)}, f32[1,216,128]{2,1,0:T(8,128)}, u32[]{:S(2)}) copy-start(f32[1,216,128]{2,1,0:T(8,128)} %param.10) | copy-start | bytes 331780
  153.3 36.2 %all-to-all-start = ((bf16[16,216,128]{2,1,0:T(8,128)(2,1)}), bf16[16,216,128]{2,1,0:T(8,128)(2,1)S(1)}, u32[]{:S(2)}, u32[]{:S(2)}) async-start(bf16[16,216,128]{2,1,0:T(8,128)(2,1)} %bitcast.5), calls=%async_computation | async-start | bytes 1769472 | tf_op jit(solution)/shard_map/all_to_all | solution.py:249
Sparse Core Ops, SparseCore 0:
  10.3 97.7 all-gather.1

commit v2 on v1

--- a/solution.py
+++ b/solution.py
@@ -39,6 +39,10 @@
         else:
             moved = jnp.where(row == HEIGHT - 1, zero, pltpu.roll(value, CELLS - 1, 0))
         store(b, moved.astype(BF16).reshape(FRAMES, WIDTH, HEIGHT, CHAN))
+
+
+def tap_rows(w, s, tap):
+    return w[s, tap * CHAN : (tap + 1) * CHAN]
 
 
 def forward_section(s, w, taps, slope, last):
@@ -55,7 +59,7 @@
             axis=1,
         )
         rhs = jnp.concatenate(
-            [w[s, (a * 3 + b) * 3 + c] for c in range(3) for b in range(3)], axis=0
+            [tap_rows(w, s, (a * 3 + b) * 3 + c) for c in range(3) for b in range(3)], axis=0
         )
         pieces.append(dot(lhs, rhs))
     total = pieces[2]
@@ -117,7 +121,7 @@
             axis=1,
         )
         rhs = jnp.concatenate(
-            [w[s, (a * 3 + 2 - b) * 3 + c] for c in range(3) for b in range(3)], axis=1
+            [tap_rows(w, s, (a * 3 + 2 - b) * 3 + c) for c in range(3) for b in range(3)], axis=1
         )
         pieces.append(
             lax.dot_general(lhs, rhs, (((1,), (1,)), ((), ())), preferred_element_type=F32)
@@ -169,25 +173,244 @@
     back[:FRAMES, WIDTH + 1] = jnp.zeros((FRAMES, HEIGHT, 3 * CHAN), BF16)
 
 
-def window_kernel(offsets, clips, w, cotangent, out, taps, back, slope, upstream):
-    segment = lax.axis_index("segment")
-    depth = segment // 2
-    mine = segment % 2
+MESH_ID = pl.DeviceIdType.MESH
+HALF = ROWS // 2
+PIECE = HALF // 4
+
+
+class Place:
+    def __init__(self):
+        segment = lax.axis_index("segment")
+        replica = lax.axis_index("replica")
+        self.z, self.hi = segment // 2, segment % 2
+        self.lo, self.y, self.core = replica // 8, replica // 2 % 4, replica % 2
+
+    def at(self, dz=0, hi=0, lo=0, dy=0, core=0):
+        z = (self.z + dz) % 4
+        y = (self.y + dy) % 4
+        own = [(self.hi + hi) % 2, (self.lo + lo) % 2, (self.core + core) % 2]
+        return (z * 2 + own[0], own[1] * 8 + y * 2 + own[2])
+
+    def partners(self):
+        away = [self.at(dz=k) for k in (1, 2, 3)]
+        across = [self.at(dz=k, hi=1, lo=1) for k in range(4)]
+        return away + across + [self.at(lo=1)] + [self.at(dy=k) for k in (1, 2, 3)] + [self.at(core=1)]
+
+
+def remote(src, dst, send, receive, device):
+    return pltpu.make_async_remote_copy(
+        src_ref=src,
+        dst_ref=dst,
+        send_sem=send,
+        recv_sem=receive,
+        device_id=device,
+        device_id_type=MESH_ID,
+    )
+
+
+def by_pair(dz, dh):
+    return (dz % 2 == 1) if dh == 0 else (dz == 0)
+
+
+class Gather:
+    def __init__(self, here, w, first_send, first_recv, pair_sem, ring_send, ring_recv, core_sem):
+        self.here, self.w = here, w
+        self.first_send, self.first_recv = first_send, first_recv
+        self.pair_sem, self.ring_send, self.ring_recv = pair_sem, ring_send, ring_recv
+        self.core_sem = core_sem
+        self.own = here.z * 2 + here.hi
+
+    def rows(self, s, start, count):
+        return self.w.at[s, pl.ds(pl.multiple_of(start, PIECE), count)]
+
+    def half(self, s, core):
+        return self.rows(s, core * HALF, HALF)
+
+    def pair_part(self, s, lo):
+        return self.rows(s, self.here.core * HALF + lo * 2 * PIECE, 2 * PIECE)
+
+    def ring_part(self, s, y):
+        return self.rows(s, self.here.core * HALF + y * PIECE, PIECE)
+
+    def firsts(self):
+        for slot, (dz, dh) in enumerate([(1, 0), (3, 0), (0, 1), (2, 0), (1, 1), (3, 1), (2, 1)]):
+            if by_pair(dz, dh):
+                part = self.pair_part(self.own, self.here.lo)
+            else:
+                part = self.ring_part(self.own, self.here.y)
+            yield remote(
+                part,
+                part,
+                self.first_send.at[slot],
+                self.first_recv.at[self.own],
+                self.here.at(dz=dz, hi=dh, lo=dh),
+            )
+
+    def start(self):
+        for copy in self.firsts():
+            copy.start()
+
+    def paired(self, s):
+        dz = (self.here.z + 4 - s // 2) % 4
+        dh = (self.here.hi + s) % 2
+        return dh, ((1 - dh) * (dz % 2) + dh * ((dz + 3) // 4 * -1 + 1)) == 1
+
+    def relay(self, s):
+        here = self.here
+        dh, paired = self.paired(s)
+
+        @pl.when(paired)
+        def _():
+            part = self.pair_part(s, (here.lo + dh) % 2)
+            remote(part, part, self.first_send.at[0], self.first_recv.at[s], here.at()).wait_recv()
+            self.pair_copy(s, dh).start()
+
+        @pl.when(jnp.logical_not(paired))
+        def _():
+            part = self.ring_part(s, here.y)
+            remote(part, part, self.first_send.at[0], self.first_recv.at[s], here.at()).wait_recv()
+            for k in (1, 3, 2):
+                self.ring_copy(s, k).start()
+
+    def pair_copy(self, s, dh):
+        part = self.pair_part(s, (self.here.lo + dh) % 2)
+        return remote(
+            part, part, self.pair_sem.at[0, s], self.pair_sem.at[1, s], self.here.at(lo=1)
+        )
+
+    def ring_copy(self, s, k):
+        part = self.ring_part(s, self.here.y)
+        return remote(
+            part, part, self.ring_send.at[s, k - 1], self.ring_recv.at[s, k - 1], self.here.at(dy=k)
+        )
+
+    def core_copy(self, s):
+        part = self.half(s, self.here.core)
+        return remote(
+            part, part, self.core_sem.at[0, s], self.core_sem.at[1, s], self.here.at(core=1)
+        )
+
+    def swap(self, s):
+        here = self.here
+        dh, paired = self.paired(s)
+
+        @pl.when(paired)
+        def _():
+            part = self.pair_part(s, (here.lo + dh + 1) % 2)
+            remote(
+                part, part, self.pair_sem.at[0, s], self.pair_sem.at[1, s], here.at(lo=1)
+            ).wait_recv()
+
+        @pl.when(jnp.logical_not(paired))
+        def _():
+            for k in (1, 3, 2):
+                part = self.ring_part(s, (here.y + 4 - k) % 4)
+                remote(
+                    part,
+                    part,
+                    self.ring_send.at[s, k - 1],
+                    self.ring_recv.at[s, k - 1],
+                    here.at(dy=k),
+                ).wait_recv()
+
+        self.core_copy(s).start()
+
+    def arrive(self, s):
+        part = self.half(s, 1 - self.here.core)
+        remote(
+            part, part, self.core_sem.at[0, s], self.core_sem.at[1, s], self.here.at(core=1)
+        ).wait_recv()
+
+    def finish(self):
+        for copy in self.firsts():
+            copy.wait_send()
+
+        def each(s, _):
+            @pl.when(s != self.own)
+            def _():
+                dh, paired = self.paired(s)
+
+                @pl.when(paired)
+                def _():
+                    self.pair_copy(s, dh).wait_send()
+
+                @pl.when(jnp.logical_not(paired))
+                def _():
+                    for k in (1, 3, 2):
+                        self.ring_copy(s, k).wait_send()
+
+                self.core_copy(s).wait_send()
+
+            return 0
+
+        lax.fori_loop(0, SECTIONS, each, 0)
+
+
+def window_kernel(
+    offsets,
+    clips,
+    weights,
+    cotangent,
+    out,
+    w,
+    taps,
+    back,
+    slope,
+    upstream,
+    load_sem,
+    first_send,
+    first_recv,
+    pair_sem,
+    ring_send,
+    ring_recv,
+    core_sem,
+):
+    here = Place()
+    gather = Gather(here, w, first_send, first_recv, pair_sem, ring_send, ring_recv, core_sem)
+    load = pltpu.make_async_copy(weights, w.at[gather.own], load_sem)
+    load.start()
+    barrier = pltpu.get_barrier_semaphore()
+    partners = here.partners()
+    for partner in partners:
+        pl.semaphore_signal(barrier, inc=1, device_id=partner, device_id_type=MESH_ID)
+    load.wait()
+    pl.semaphore_wait(barrier, len(partners))
+    gather.start()
+
     clear_edges(taps, back)
-    crop(clips.at[mine], offsets[mine, 0], offsets[mine, 1], taps)
-    reorder(cotangent.at[mine], upstream)
-
-    def forward(s, _):
-        forward_section(s, w, taps, slope, SECTIONS - 1)
+    crop(clips.at[here.hi], offsets[here.hi, 0], offsets[here.hi, 1], taps)
+    reorder(cotangent.at[here.hi], upstream)
+
+    def forward(tick, _):
+        @pl.when((tick < SECTIONS) & (tick != gather.own))
+        def _():
+            gather.relay(tick)
+
+        later = tick - 1
+
+        @pl.when((later >= 0) & (later < SECTIONS) & (later != gather.own))
+        def _():
+            gather.swap(later)
+
+        s = tick - 2
+
+        @pl.when(s >= 0)
+        def _():
+            @pl.when(s != gather.own)
+            def _():
+                gather.arrive(s)
+
+            forward_section(s, w, taps, slope, SECTIONS - 1)
+
         return 0
 
-    lax.fori_loop(0, SECTIONS, forward, 0)
+    lax.fori_loop(0, SECTIONS + 2, forward, 0)
 
     def backward(i, _):
         s = SECTIONS - 1 - i
         shifted_delta(s, upstream, slope, back)
 
-        @pl.when(s // 2 == depth)
+        @pl.when(s // 2 == here.z)
         def _():
             def put(tap, block):
                 out[s % 2, tap] = block.astype(BF16)
@@ -201,23 +424,40 @@
         return 0
 
     lax.fori_loop(0, SECTIONS, backward, 0)
-
-
-def window(offsets, clips, w, cotangent):
+    gather.finish()
+
+
+def window(offsets, clips, weights, cotangent):
     vmem = pl.BlockSpec(memory_space=pltpu.VMEM)
+    dma = pltpu.SemaphoreType.DMA
     return pl.pallas_call(
         window_kernel,
         out_shape=jax.ShapeDtypeStruct((2, TAPS, CHAN, CHAN), BF16),
-        in_specs=[pl.BlockSpec(memory_space=pltpu.SMEM), vmem, vmem, vmem],
+        in_specs=[
+            pl.BlockSpec(memory_space=pltpu.SMEM),
+            vmem,
+            pl.BlockSpec(memory_space=pl.ANY),
+            vmem,
+        ],
         out_specs=vmem,
         scratch_shapes=[
+            pltpu.VMEM((SECTIONS, ROWS, CHAN), BF16),
             pltpu.VMEM((SECTIONS, FRAMES + 2, WIDTH + 2, HEIGHT, 3 * CHAN), BF16),
             pltpu.VMEM((FRAMES + 2, WIDTH + 2, HEIGHT, 3 * CHAN), BF16),
             pltpu.VMEM((SECTIONS, CELLS, CHAN), F32),
             pltpu.VMEM((CELLS, CHAN), F32),
+            dma,
+            dma((7,)),
+            dma((SECTIONS,)),
+            dma((2, SECTIONS)),
+            dma((SECTIONS, 3)),
+            dma((SECTIONS, 3)),
+            dma((2, SECTIONS)),
         ],
-        compiler_params=pltpu.CompilerParams(vmem_limit_bytes=56 << 20),
-    )(offsets, clips, w, cotangent)
+        compiler_params=pltpu.CompilerParams(
+            vmem_limit_bytes=56 << 20, collective_id=0, has_side_effects=True
+        ),
+    )(offsets, clips, weights, cotangent)
 
 
 def adam_rows(weights, moment, second, stale_grads):
@@ -234,11 +474,10 @@
 def shards(clips, offsets, weights, moment, second, stale_grads, cotangent):
     micro = clips.shape[0]
     mine = lax.axis_index("segment") % 2
-    gathered = lax.all_gather(weights[0], "segment", axis=0)
     partial = window(
         offsets,
         clips.reshape(micro, FRAMES, -1, CHAN),
-        gathered.reshape(SECTIONS, TAPS, CHAN, CHAN),
+        weights[0],
         cotangent.reshape(micro, FRAMES, PLANE, CHAN),
     )
     keep = lax.dynamic_index_in_dim(partial, mine, 0, keepdims=False)

time: 198 us -> 129 us (0.65)
  the two profiles are of different devices: /device:TPU:1 before, /device:TPU:71 now
where the time goes in v2:
time: 129 us
  Pallas kernels  67.4 us (52%)
  blocking collectives  27.8 us (22%)
  waiting for transfers between devices  22.6 us (18%)
  starting transfers between devices  4.47 us (3%)
  other arithmetic  3.61 us (3%)
  local copies, waits for them, and re-layouts  2.29 us (2%)
    pallas_call x1, Pallas kernels, window(): pl.pallas_call(window_kernel, out_shape=jax.ShapeDtypeStruct((2, TAPS, CH...  67.4 us
    all_gather x1, blocking collectives, adam_rows(): whole = lax.all_gather(fresh, 'replica', axis=0, tiled=True)  27.8 us
    ppermute x1, waiting for transfers between devices, shards(): taken = lax.ppermute(give, 'segment', [(s, s ^ 1) for s in range(SECTIONS)])  22.6 us
    all_to_all x1, starting transfers between devices, shards(): lax.all_to_all(pair.reshape(count, -1, CHAN), 'replica', 0, 0, tiled=True)  4.39 us
  transfers between devices with their start and end apart: 2, of which 1 were waited for; matrix products, arithmetic and copies ran while one was open for 1% of the time, Pallas kernels for 0%

profile of v2, /device:TPU:71, one launch (start us, length us, event | category | flops | bytes accessed | tf_op | source)
XLA Modules:
  0.0 128.8 jit_solution(9840001414327116652)
XLA Ops:
  0.6 67.4 %shard_map.102 = bf16[2,27,128,128]{3,2,1,0:T(8,128)(2,1)} custom-call(s32[2,2]{1,0:T(2,128)} %offsets.1, bf16[2,4,384,128]{3,2,1,0:T(8,128)(2,1)} %bitcast.35, bf16[3456,128]{1,0:T(8,128)(2,1)} %bitcast.34, bf16[2,4,128,128]{3,2,1,0:T(8,128)(2,1)} %bitcast.36), custom_call_target="tpu_custom_call" | custom-call | tf_op jit(solution)/shard_map/pallas_call | solution.py:433
  68.0 0.0 copy-start
  68.0 1.4 %dynamic-slice_bitcast_fusion = bf16[27,128,128]{2,1,0:T(8,128)(2,1)S(1)} fusion(bf16[2,27,128,128]{3,2,1,0:T(8,128)(2,1)} %shard_map.102, s32[]{:T(128)S(6)} %select_n.19), kind=kLoop, calls=%fused_computation.3 | loop fusion | bytes 1769476 | tf_op jit(solution)/shard_map/jit(dynamic_index_in_dim)/squeeze | solution.py:484
  69.4 0.1 collective-permute-start
  69.5 22.6 %collective-permute-done = bf16[27,128,128]{2,1,0:T(8,128)(2,1)S(1)} collective-permute-done((bf16[27,128,128]{2,1,0:T(8,128)(2,1)S(1)}, bf16[27,128,128]{2,1,0:T(8,128)(2,1)S(1)}, u32[]{:S(2)}, u32[]{:S(2)}) %collective-permute-start) | collective-permute-done | bytes 884768 | tf_op jit(solution)/shard_map/ppermute | solution.py:485
  92.1 0.0 copy-done
  92.1 0.0 copy-start.1
  92.1 0.0 copy-start.2
  92.1 0.0 copy-start.3
  92.1 1.2 fusion
  93.3 4.4 %all-to-all-start = ((bf16[16,216,128]{2,1,0:T(8,128)(2,1)}), bf16[16,216,128]{2,1,0:T(8,128)(2,1)S(1)}, u32[]{:S(2)}, u32[]{:S(2)}) async-start(bf16[16,216,128]{2,1,0:T(8,128)(2,1)} %bitcast.5), calls=%async_computation | async-start | bytes 1769472 | tf_op jit(solution)/shard_map/all_to_all | solution.py:488
  97.7 0.0 copy-done.1
  97.7 0.0 copy-done.2
  97.7 0.0 copy-done.3
  97.7 0.9 fusion.9
  98.6 27.8 %all_gather.3 = bf16[3456,128]{1,0:T(8,128)(2,1)S(1)} all-gather(bf16[216,128]{1,0:T(8,128)(2,1)S(1)} %fusion.9), channel_id=1, replica_groups=mesh['segment'=8,'replica'=16] {'replica'}, dimensions={0}, use_global_device_ids=true | all-gather | bytes 940032 | tf_op jit(solution)/shard_map/all_gather | solution.py:470
  126.4 0.7 fusion.1
  127.2 0.0 all-to-all-done
  127.2 0.8 convert_reduce_fusion
  127.9 0.9 copy.12
Async XLA Ops:
  68.0 24.0 %copy-start = (bf16[2,27,128,128]{3,2,1,0:T(8,128)(2,1)S(1)}, bf16[2,27,128,128]{3,2,1,0:T(8,128)(2,1)}, u32[]{:S(2)}) copy-start(bf16[2,27,128,128]{3,2,1,0:T(8,128)(2,1)} %shard_map.102) | copy-start | bytes 5308420
  69.4 22.7 %collective-permute-start = (bf16[27,128,128]{2,1,0:T(8,128)(2,1)S(1)}, bf16[27,128,128]{2,1,0:T(8,128)(2,1)S(1)}, u32[]{:S(2)}, u32[]{:S(2)}) collective-permute-start(bf16[27,128,128]{2,1,0:T(8,128)(2,1)S(1)} %dynamic-slice_bitcast_fusion), channel_id=1, source_target_pairs={{0,16},{16,0},{32,48},{48,32},{64,80},{80,64},{96,112},{112,96},{1... | collective-permute-start | bytes 2654216 | tf_op jit(solution)/shard_map/ppermute | solution.py:485
  92.1 5.6 %copy-start.1 = (f32[1,216,128]{2,1,0:T(8,128)S(1)}, f32[1,216,128]{2,1,0:T(8,128)}, u32[]{:S(2)}) copy-start(f32[1,216,128]{2,1,0:T(8,128)} %param.12) | copy-start | bytes 331780
  92.1 5.6 %copy-start.2 = (f32[1,216,128]{2,1,0:T(8,128)S(1)}, f32[1,216,128]{2,1,0:T(8,128)}, u32[]{:S(2)}) copy-start(f32[1,216,128]{2,1,0:T(8,128)} %param.11) | copy-start | bytes 331780
  92.1 5.6 %copy-start.3 = (f32[1,216,128]{2,1,0:T(8,128)S(1)}, f32[1,216,128]{2,1,0:T(8,128)}, u32[]{:S(2)}) copy-start(f32[1,216,128]{2,1,0:T(8,128)} %param.10) | copy-start | bytes 331780
  93.3 33.9 %all-to-all-start = ((bf16[16,216,128]{2,1,0:T(8,128)(2,1)}), bf16[16,216,128]{2,1,0:T(8,128)(2,1)S(1)}, u32[]{:S(2)}, u32[]{:S(2)}) async-start(bf16[16,216,128]{2,1,0:T(8,128)(2,1)} %bitcast.5), calls=%async_computation | async-start | bytes 1769472 | tf_op jit(solution)/shard_map/all_to_all | solution.py:488

commit v3 on v2

--- a/solution.py
+++ b/solution.py
@@ -176,6 +176,7 @@
 MESH_ID = pl.DeviceIdType.MESH
 HALF = ROWS // 2
 PIECE = HALF // 4
+SHARD = ROWS // 16
 
 
 class Place:
@@ -194,7 +195,7 @@
     def partners(self):
         away = [self.at(dz=k) for k in (1, 2, 3)]
         across = [self.at(dz=k, hi=1, lo=1) for k in range(4)]
-        return away + across + [self.at(lo=1)] + [self.at(dy=k) for k in (1, 2, 3)] + [self.at(core=1)]
+        return away + across + [self.at(lo=1), self.at(hi=1)] + [self.at(dy=k) for k in (1, 2, 3)] + [self.at(core=1)]
 
 
 def remote(src, dst, send, receive, device):
@@ -346,17 +347,169 @@
         lax.fori_loop(0, SECTIONS, each, 0)
 
 
+class Exchange:
+    def __init__(self, here, total, give, taken, summed, ring, kept, crossed, sems):
+        self.here = here
+        self.total, self.give, self.taken, self.summed = total, give, taken, summed
+        self.ring, self.kept, self.crossed = ring, kept, crossed
+        self.core_sem, self.ring_send, self.ring_recv, self.cross_send, self.cross_recv = sems
+
+    def shard(self, i, j, core):
+        start = pl.multiple_of((2 * j + core) * SHARD, 8)
+        return self.total[i, pl.ds(start, SHARD)]
+
+    def core_copy(self, i):
+        return remote(
+            self.give.at[i],
+            self.taken.at[i],
+            self.core_sem.at[0, i],
+            self.core_sem.at[1, i],
+            self.here.at(core=1),
+        )
+
+    def to_core(self, i):
+        for j in range(8):
+            self.give[i, j] = self.shard(i, j, 1 - self.here.core).astype(BF16)
+        self.core_copy(i).start()
+
+    def ring_copy(self, i, k):
+        return remote(
+            self.summed.at[i, :, (self.here.y + k) % 4],
+            self.ring.at[i, k - 1],
+            self.ring_send.at[i, k - 1],
+            self.ring_recv.at[i, k - 1],
+            self.here.at(dy=k),
+        )
+
+    def to_ring(self, i):
+        self.core_copy(i).wait_recv()
+        for j in range(8):
+            both = self.shard(i, j, self.here.core) + self.taken[i, j].astype(F32)
+            self.summed[i, j // 4, j % 4] = both.astype(BF16)
+        for k in (2, 1, 3):
+            self.ring_copy(i, k).start()
+
+    def cross_copy(self, i, slot):
+        hi, lo = ((0, 1), (1, 0), (1, 1))[slot]
+        return remote(
+            self.kept.at[i, (self.here.lo + lo) % 2],
+            self.crossed.at[slot],
+            self.cross_send.at[slot],
+            self.cross_recv.at[slot],
+            self.here.at(hi=hi, lo=lo),
+        )
+
+    def to_cross(self, i):
+        for k in (1, 3, 2):
+            self.ring_copy(i, k).wait_recv()
+        for lo in range(2):
+            value = self.summed[i, lo, self.here.y].astype(F32)
+            for k in range(3):
+                value = value + self.ring[i, k, lo].astype(F32)
+            self.kept[i, lo] = value.astype(BF16)
+
+        @pl.when(self.here.hi == i)
+        def _():
+            self.cross_copy(i, 0).start()
+
+        @pl.when(self.here.hi != i)
+        def _():
+            self.cross_copy(i, 1).start()
+            self.cross_copy(i, 2).start()
+
+    def finish(self, grads):
+        for slot in range(3):
+            self.cross_copy(0, slot).wait_recv()
+        value = self.kept[self.here.hi, self.here.lo].astype(F32)
+        for slot in range(3):
+            value = value + self.crossed[slot].astype(F32)
+        grads[...] = value
+        for i in range(2):
+            self.core_copy(i).wait_send()
+            for k in (1, 2, 3):
+                self.ring_copy(i, k).wait_send()
+        for slot in range(3):
+            self.cross_copy(0, slot).wait_send()
+
+
+class Renewal:
+    def __init__(self, here, fresh, ring_sem, pair_sem, core_sem):
+        self.here, self.fresh = here, fresh
+        self.ring_sem, self.pair_sem, self.core_sem = ring_sem, pair_sem, core_sem
+
+    def compute(self, rows, moment, second, stale, new_moment, new_second):
+        here = self.here
+        first = beta_one * moment[...] + (1.0 - beta_one) * stale[...]
+        square = beta_two * second[...] + (1.0 - beta_two) * stale[...] * stale[...]
+        new_moment[...] = first
+        new_second[...] = square
+        step = learn_rate * first / (jnp.sqrt(square) + adam_eps)
+        self.fresh[here.lo, here.y, here.core] = (rows[...].astype(F32) - step).astype(BF16)
+
+    def ring_copy(self, k, back=0):
+        part = self.fresh.at[self.here.lo, (self.here.y + back) % 4, self.here.core]
+        return remote(
+            part, part, self.ring_sem.at[0, k - 1], self.ring_sem.at[1, k - 1], self.here.at(dy=k)
+        )
+
+    def pair_copy(self, lo=0):
+        part = self.fresh.at[(self.here.lo + lo) % 2, :, self.here.core]
+        return remote(part, part, self.pair_sem.at[0], self.pair_sem.at[1], self.here.at(lo=1))
+
+    def core_copy(self, core=0):
+        part = self.fresh.at[:, :, (self.here.core + core) % 2]
+        return remote(part, part, self.core_sem.at[0], self.core_sem.at[1], self.here.at(core=1))
+
+    def to_ring(self):
+        for k in (2, 1, 3):
+            self.ring_copy(k).start()
+
+    def to_pair(self):
+        for k in (1, 3, 2):
+            self.ring_copy(k, 4 - k).wait_recv()
+        self.pair_copy().start()
+
+    def to_core(self):
+        self.pair_copy(1).wait_recv()
+        self.core_copy().start()
+
+    def arrive(self):
+        self.core_copy(1).wait_recv()
+
+    def finish(self):
+        for k in (1, 2, 3):
+            self.ring_copy(k).wait_send()
+        self.pair_copy().wait_send()
+        self.core_copy().wait_send()
+
+
 def window_kernel(
     offsets,
     clips,
     weights,
+    shards16,
+    moment,
+    second,
+    stale,
     cotangent,
-    out,
+    grads,
+    new_moment,
+    new_second,
+    new_weights,
     w,
     taps,
     back,
     slope,
     upstream,
+    rows,
+    fresh,
+    total,
+    give,
+    taken,
+    summed,
+    ring,
+    kept,
+    crossed,
     load_sem,
     first_send,
     first_recv,
@@ -364,11 +517,35 @@
     ring_send,
     ring_recv,
     core_sem,
+    sum_core,
+    sum_ring_send,
+    sum_ring_recv,
+    cross_send,
+    cross_recv,
+    renew_ring,
+    renew_pair,
+    renew_core,
 ):
     here = Place()
     gather = Gather(here, w, first_send, first_recv, pair_sem, ring_send, ring_recv, core_sem)
-    load = pltpu.make_async_copy(weights, w.at[gather.own], load_sem)
+    exchange = Exchange(
+        here,
+        total,
+        give,
+        taken,
+        summed,
+        ring,
+        kept,
+        crossed,
+        (sum_core, sum_ring_send, sum_ring_recv, cross_send, cross_recv),
+    )
+    renewal = Renewal(here, fresh, renew_ring, renew_pair, renew_core)
+    load = pltpu.make_async_copy(weights, w.at[gather.own], load_sem.at[0])
     load.start()
+    own_rows = pltpu.make_async_copy(
+        shards16.at[here.lo * 8 + here.y * 2 + here.core], rows, load_sem.at[1]
+    )
+    own_rows.start()
     barrier = pltpu.get_barrier_semaphore()
     partners = here.partners()
     for partner in partners:
@@ -380,6 +557,8 @@
     clear_edges(taps, back)
     crop(clips.at[here.hi], offsets[here.hi, 0], offsets[here.hi, 1], taps)
     reorder(cotangent.at[here.hi], upstream)
+    own_rows.wait()
+    renewal.compute(rows, moment, second, stale, new_moment, new_second)
 
     def forward(tick, _):
         @pl.when((tick < SECTIONS) & (tick != gather.own))
@@ -405,90 +584,131 @@
         return 0
 
     lax.fori_loop(0, SECTIONS + 2, forward, 0)
+    renewal.to_ring()
 
     def backward(i, _):
         s = SECTIONS - 1 - i
         shifted_delta(s, upstream, slope, back)
 
+        @pl.when(s == 2 * here.z)
+        def _():
+            exchange.to_ring(1)
+
         @pl.when(s // 2 == here.z)
         def _():
             def put(tap, block):
-                out[s % 2, tap] = block.astype(BF16)
+                total[s % 2, tap * CHAN : (tap + 1) * CHAN] = block
 
             weight_grad(s, taps, back, put)
+            exchange.to_core(s % 2)
+
+        @pl.when(s == 2 * here.z)
+        def _():
+            exchange.to_cross(1)
 
         @pl.when(s > 0)
         def _():
             input_grad(s, w, back, upstream)
 
+        @pl.when(s == 5)
+        def _():
+            renewal.to_pair()
+
+        @pl.when(s == 3)
+        def _():
+            renewal.to_core()
+
         return 0
 
     lax.fori_loop(0, SECTIONS, backward, 0)
+    renewal.arrive()
+    store = pltpu.make_async_copy(fresh, new_weights, load_sem.at[0])
+    store.start()
+    exchange.to_ring(0)
+    exchange.to_cross(0)
+    exchange.finish(grads)
+    renewal.finish()
     gather.finish()
-
-
-def window(offsets, clips, weights, cotangent):
+    store.wait()
+
+
+def window(offsets, clips, weights, moment, second, stale, cotangent):
     vmem = pl.BlockSpec(memory_space=pltpu.VMEM)
+    away = pl.BlockSpec(memory_space=pl.ANY)
     dma = pltpu.SemaphoreType.DMA
+    shard = jax.ShapeDtypeStruct((SHARD, CHAN), F32)
     return pl.pallas_call(
         window_kernel,
-        out_shape=jax.ShapeDtypeStruct((2, TAPS, CHAN, CHAN), BF16),
+        out_shape=(shard, shard, shard, jax.ShapeDtypeStruct((2, 4, 2, SHARD, CHAN), BF16)),
         in_specs=[
             pl.BlockSpec(memory_space=pltpu.SMEM),
             vmem,
-            pl.BlockSpec(memory_space=pl.ANY),
+            away,
+            away,
+            vmem,
+            vmem,
+            vmem,
             vmem,
         ],
-        out_specs=vmem,
+        out_specs=(vmem, vmem, vmem, away),
         scratch_shapes=[
             pltpu.VMEM((SECTIONS, ROWS, CHAN), BF16),
             pltpu.VMEM((SECTIONS, FRAMES + 2, WIDTH + 2, HEIGHT, 3 * CHAN), BF16),
             pltpu.VMEM((FRAMES + 2, WIDTH + 2, HEIGHT, 3 * CHAN), BF16),
             pltpu.VMEM((SECTIONS, CELLS, CHAN), F32),
             pltpu.VMEM((CELLS, CHAN), F32),
-            dma,
+            pltpu.VMEM((SHARD, CHAN), BF16),
+            pltpu.VMEM((2, 4, 2, SHARD, CHAN), BF16),
+            pltpu.VMEM((2, ROWS, CHAN), F32),
+            pltpu.VMEM((2, 8, SHARD, CHAN), BF16),
+            pltpu.VMEM((2, 8, SHARD, CHAN), BF16),
+            pltpu.VMEM((2, 2, 4, SHARD, CHAN), BF16),
+            pltpu.VMEM((2, 3, 2, SHARD, CHAN), BF16),
+            pltpu.VMEM((2, 2, SHARD, CHAN), BF16),
+            pltpu.VMEM((3, SHARD, CHAN), BF16),
+            dma((2,)),
             dma((7,)),
             dma((SECTIONS,)),
             dma((2, SECTIONS)),
             dma((SECTIONS, 3)),
             dma((SECTIONS, 3)),
             dma((2, SECTIONS)),
+            dma((2, 2)),
+            dma((2, 3)),
+            dma((2, 3)),
+            dma((3,)),
+            dma((3,)),
+            dma((2, 3)),
+            dma((2,)),
+            dma((2,)),
         ],
         compiler_params=pltpu.CompilerParams(
             vmem_limit_bytes=56 << 20, collective_id=0, has_side_effects=True
         ),
-    )(offsets, clips, weights, cotangent)
-
-
-def adam_rows(weights, moment, second, stale_grads):
-    rows = moment.shape[1]
-    start = lax.axis_index("replica") * rows
-    local = lax.dynamic_slice_in_dim(weights[0], start, rows, 0).astype(F32)
-    first_new = beta_one * moment[0] + (1.0 - beta_one) * stale_grads[0]
-    second_new = beta_two * second[0] + (1.0 - beta_two) * stale_grads[0] * stale_grads[0]
-    fresh = (local - learn_rate * first_new / (jnp.sqrt(second_new) + adam_eps)).astype(BF16)
-    whole = lax.all_gather(fresh, "replica", axis=0, tiled=True)
-    return (first_new[None], second_new[None], whole[None])
+    )(
+        offsets,
+        clips,
+        weights,
+        weights.reshape(16, SHARD, CHAN),
+        moment,
+        second,
+        stale,
+        cotangent,
+    )
 
 
 def shards(clips, offsets, weights, moment, second, stale_grads, cotangent):
     micro = clips.shape[0]
-    mine = lax.axis_index("segment") % 2
-    partial = window(
+    grads, first_new, second_new, fresh = window(
         offsets,
         clips.reshape(micro, FRAMES, -1, CHAN),
         weights[0],
+        moment[0],
+        second[0],
+        stale_grads[0],
         cotangent.reshape(micro, FRAMES, PLANE, CHAN),
     )
-    keep = lax.dynamic_index_in_dim(partial, mine, 0, keepdims=False)
-    give = lax.dynamic_index_in_dim(partial, 1 - mine, 0, keepdims=False)
-    taken = lax.ppermute(give, "segment", [(s, s ^ 1) for s in range(SECTIONS)])
-    pair = (keep.astype(F32) + taken.astype(F32)).astype(BF16)
-    count = lax.axis_size("replica")
-    pieces = lax.all_to_all(pair.reshape(count, -1, CHAN), "replica", 0, 0, tiled=True)
-    grads = jnp.sum(pieces.astype(F32), axis=0)
-    first_new, second_new, whole = adam_rows(weights, moment, second, stale_grads)
-    return (grads[None], first_new, second_new, whole)
+    return (grads[None], first_new[None], second_new[None], fresh.reshape(1, ROWS, CHAN))
 
 
 def solution(mesh):

time: 129 us -> 93.5 us (0.72)
  the two profiles are of different devices: /device:TPU:71 before, /device:TPU:1 now
where the time goes in v3:
time: 93.5 us; the launch traced here: 92.4 us
  Pallas kernels  86.4 us (92%)
  local copies, waits for them, and re-layouts  5.3 us (6%)
    pallas_call x1, Pallas kernels, window(): pl.pallas_call(window_kernel, out_shape=(shard, shard, shard, jax.ShapeDt...  86.4 us
    unnamed x8, local copies, waits for them, and re-layouts  5.3 us

profile of v3, /device:TPU:1, one launch (start us, length us, event | category | flops | bytes accessed | tf_op | source)
XLA Modules:
  0.0 92.4 jit_solution(9034382147623256891)
XLA Ops:
  0.6 86.4 %shard_map.102 = (f32[216,128]{1,0:T(8,128)}, f32[216,128]{1,0:T(8,128)}, f32[216,128]{1,0:T(8,128)}, bf16[2,4,2,216,128]{4,3,2,1,0:T(8,128)(2,1)}) custom-call(s32[2,2]{1,0:T(2,128)} %offsets.1, bf16[2,4,384,128]{3,2,1,0:T(8,128)(2,1)} %bitcast.14, bf16[3456,128]{1,0:T(8,128)(2,1)} %bitcast.11, bf16[16,216,128]{2,1,0:T(8,128)(2,1)} %bitcast.12, ...), custom_call_target="tpu_custom_call" | custom-call | tf_op jit(solution)/shard_map/pallas_call | solution.py:640
  87.1 0.0 copy-start.1
  87.1 1.6 %copy.15 = f32[1,216,128]{2,1,0:T(8,128)} copy(f32[1,216,128]{2,1,0:T(8,128)} %bitcast.18) | data formatting | bytes 221184
  88.7 0.0 copy-done.1
  88.7 0.0 copy-start
  88.7 0.6 copy.16
  89.3 0.3 copy-done
  89.6 0.6 copy.17
  90.3 2.1 %copy.18 = bf16[1,3456,128]{2,1,0:T(8,128)(2,1)} copy(bf16[1,3456,128]{2,1,0:T(8,128)(2,1)} %bitcast.13) | data formatting | bytes 1769472
Async XLA Ops:
  87.1 1.6 %copy-start.1 = (f32[216,128]{1,0:T(8,128)S(1)}, f32[216,128]{1,0:T(8,128)}, u32[]{:S(2)}) copy-start(f32[216,128]{1,0:T(8,128)} %get-tuple-element.9) | copy-start | bytes 331780
  88.7 0.9 %copy-start = (f32[216,128]{1,0:T(8,128)S(1)}, f32[216,128]{1,0:T(8,128)}, u32[]{:S(2)}) copy-start(f32[216,128]{1,0:T(8,128)} %get-tuple-element.10) | copy-start | bytes 331780

commit v4 on v3

--- a/solution.py
+++ b/solution.py
@@ -45,29 +45,37 @@
     return w[s, tap * CHAN : (tap + 1) * CHAN]
 
 
+def dot_turned(a, b):
+    return lax.dot_general(a, b, (((1,), (1,)), ((), ())), preferred_element_type=F32)
+
+
+def tap_block(w, s, times, turn, axis):
+    columns = []
+    for a in times:
+        taps = [turn(b, c) for c in range(3) for b in range(3)]
+        columns.append(
+            jnp.concatenate([tap_rows(w, s, (a * 3 + b) * 3 + c) for b, c in taps], axis=axis)
+        )
+    return jnp.concatenate(columns, axis=1 - axis)
+
+
+def field_columns(field):
+    padded = field.reshape(FRAMES, WIDTH + 2, HEIGHT, 3 * CHAN)
+    return jnp.concatenate(
+        [padded[:, c : c + WIDTH].reshape(CELLS, 3 * CHAN) for c in range(3)], axis=1
+    )
+
+
 def forward_section(s, w, taps, slope, last):
-    total = None
-    pieces = []
-    for a in range(3):
-        frames = 2 + a
-        first = FRAMES - frames
-        lhs = jnp.concatenate(
-            [
-                taps[s, a + first : a + FRAMES, c : c + WIDTH].reshape(frames * PLANE, 3 * CHAN)
-                for c in range(3)
-            ],
-            axis=1,
-        )
-        rhs = jnp.concatenate(
-            [tap_rows(w, s, (a * 3 + b) * 3 + c) for c in range(3) for b in range(3)], axis=0
-        )
-        pieces.append(dot(lhs, rhs))
-    total = pieces[2]
-    total = jnp.concatenate(
+    field = taps[s].reshape(FRAMES * (WIDTH + 2) * HEIGHT, 3 * CHAN)
+    lhs = field_columns(field)
+    late = dot(lhs, tap_block(w, s, (1, 2), lambda b, c: (b, c), 0))
+    early = dot(lhs[: 2 * PLANE], tap_block(w, s, (0,), lambda b, c: (b, c), 0))
+    total = late[:, CHAN:] + jnp.concatenate(
         [
-            total[:PLANE],
-            total[PLANE : 2 * PLANE] + pieces[1][:PLANE],
-            total[2 * PLANE :] + pieces[1][PLANE:] + pieces[0],
+            jnp.zeros((PLANE, CHAN), F32),
+            late[:PLANE, :CHAN],
+            late[PLANE : 3 * PLANE, :CHAN] + early,
         ],
         axis=0,
     )
@@ -78,7 +86,7 @@
     @pl.when(s < last)
     def _():
         def store(b, moved):
-            taps[s + 1, 2:, 1 : 1 + WIDTH, :, b * CHAN : (b + 1) * CHAN] = moved
+            taps[s + 1, :, 1 : 1 + WIDTH, :, b * CHAN : (b + 1) * CHAN] = moved
 
         store_shifted(store, pre * sigma)
 
@@ -87,31 +95,18 @@
     delta = upstream[...] * slope[s]
 
     def store(b, moved):
-        back[:FRAMES, 1 : 1 + WIDTH, :, b * CHAN : (b + 1) * CHAN] = moved
+        back[:, 1 : 1 + WIDTH, :, b * CHAN : (b + 1) * CHAN] = moved
 
     store_shifted(store, delta)
 
 
 def weight_grad(s, taps, back, put):
-    field = taps[s, 2:, 1 : 1 + WIDTH, :, CHAN : 2 * CHAN].reshape(CELLS, CHAN)
+    field = taps[s, :, 1 : 1 + WIDTH, :, CHAN : 2 * CHAN].reshape(CELLS, CHAN)
     turned = field.astype(F32).T.astype(BF16)
     for a in range(3):
         frames = 2 + a
         lhs = turned[:, : frames * PLANE]
-        for c in range(3):
-            rhs = back[2 - a : 2 - a + frames, 2 - c : 2 - c + WIDTH].reshape(
-                frames * PLANE, 3 * CHAN
-            )
-            out = dot(lhs, rhs) * GRAD_SCALE
-            for b in range(3):
-                put((a * 3 + b) * 3 + c, out[:, (2 - b) * CHAN : (3 - b) * CHAN])
-
-
-def input_grad(s, w, back, upstream):
-    pieces = []
-    for a in range(3):
-        frames = 2 + a
-        lhs = jnp.concatenate(
+        rhs = jnp.concatenate(
             [
                 back[2 - a : 2 - a + frames, 2 - c : 2 - c + WIDTH].reshape(
                     frames * PLANE, 3 * CHAN
@@ -120,18 +115,25 @@
             ],
             axis=1,
         )
-        rhs = jnp.concatenate(
-            [tap_rows(w, s, (a * 3 + 2 - b) * 3 + c) for c in range(3) for b in range(3)], axis=1
-        )
-        pieces.append(
-            lax.dot_general(lhs, rhs, (((1,), (1,)), ((), ())), preferred_element_type=F32)
-        )
-    total = pieces[2]
-    total = jnp.concatenate(
+        out = dot(lhs, rhs) * GRAD_SCALE
+        for c in range(3):
+            for b in range(3):
+                first = (c * 3 + 2 - b) * CHAN
+                put((a * 3 + b) * 3 + c, out[:, first : first + CHAN])
+
+
+def input_grad(s, w, back, upstream):
+    field = back[...].reshape(FRAMES * (WIDTH + 2) * HEIGHT, 3 * CHAN)
+    lhs = field_columns(field)
+    flip = lambda b, c: (2 - b, 2 - c)
+    late = dot_turned(lhs, tap_block(w, s, (1, 2), flip, 1))
+    early = dot_turned(lhs[2 * PLANE :], tap_block(w, s, (0,), flip, 1))
+    total = late[:, CHAN:] + jnp.concatenate(
         [
-            total[: 2 * PLANE] + pieces[1][: 2 * PLANE] + pieces[0],
-            total[2 * PLANE : 3 * PLANE] + pieces[1][2 * PLANE :],
-            total[3 * PLANE :],
+            late[PLANE : 2 * PLANE, :CHAN] + early[:PLANE],
+            late[2 * PLANE : 3 * PLANE, :CHAN] + early[PLANE:],
+            late[3 * PLANE :, :CHAN],
+            jnp.zeros((PLANE, CHAN), F32),
         ],
         axis=0,
     )
@@ -147,7 +149,7 @@
     field = jnp.concatenate([dot(pick, clip[t]) for t in range(FRAMES)], axis=0)
 
     def store(b, moved):
-        taps[0, 2:, 1 : 1 + WIDTH, :, b * CHAN : (b + 1) * CHAN] = moved
+        taps[0, :, 1 : 1 + WIDTH, :, b * CHAN : (b + 1) * CHAN] = moved
 
     store_shifted(store, field)
 
@@ -161,16 +163,16 @@
 
 
 def clear_edges(taps, back):
+    edge = jnp.zeros((FRAMES, HEIGHT, 3 * CHAN), BF16)
+
     def wipe(s, _):
-        taps[s, :2] = jnp.zeros((2, WIDTH + 2, HEIGHT, 3 * CHAN), BF16)
-        taps[s, 2:, 0] = jnp.zeros((FRAMES, HEIGHT, 3 * CHAN), BF16)
-        taps[s, 2:, WIDTH + 1] = jnp.zeros((FRAMES, HEIGHT, 3 * CHAN), BF16)
+        taps[s, :, 0] = edge
+        taps[s, :, WIDTH + 1] = edge
         return 0
 
     lax.fori_loop(0, SECTIONS, wipe, 0)
-    back[FRAMES:] = jnp.zeros((2, WIDTH + 2, HEIGHT, 3 * CHAN), BF16)
-    back[:FRAMES, 0] = jnp.zeros((FRAMES, HEIGHT, 3 * CHAN), BF16)
-    back[:FRAMES, WIDTH + 1] = jnp.zeros((FRAMES, HEIGHT, 3 * CHAN), BF16)
+    back[:, 0] = edge
+    back[:, WIDTH + 1] = edge
 
 
 MESH_ID = pl.DeviceIdType.MESH
@@ -209,118 +211,121 @@
     )
 
 
-def by_pair(dz, dh):
-    return (dz % 2 == 1) if dh == 0 else (dz == 0)
+DIRECT, PAIR, RING, NEAR = range(4)
+MODES = {
+    (1, 0): DIRECT,
+    (3, 0): DIRECT,
+    (2, 0): NEAR,
+    (0, 1): PAIR,
+    (1, 1): RING,
+    (3, 1): RING,
+    (2, 1): NEAR,
+}
+ORDER = ((2, 0), (2, 1), (1, 0), (3, 0), (0, 1), (1, 1), (3, 1))
 
 
 class Gather:
-    def __init__(self, here, w, first_send, first_recv, pair_sem, ring_send, ring_recv, core_sem):
+    def __init__(self, here, w, first_send, first_recv, relay_send, relay_recv, core_sem):
         self.here, self.w = here, w
         self.first_send, self.first_recv = first_send, first_recv
-        self.pair_sem, self.ring_send, self.ring_recv = pair_sem, ring_send, ring_recv
+        self.relay_send, self.relay_recv = relay_send, relay_recv
         self.core_sem = core_sem
         self.own = here.z * 2 + here.hi
 
-    def rows(self, s, start, count):
-        return self.w.at[s, pl.ds(pl.multiple_of(start, PIECE), count)]
-
-    def half(self, s, core):
-        return self.rows(s, core * HALF, HALF)
-
-    def pair_part(self, s, lo):
-        return self.rows(s, self.here.core * HALF + lo * 2 * PIECE, 2 * PIECE)
-
-    def ring_part(self, s, y):
-        return self.rows(s, self.here.core * HALF + y * PIECE, PIECE)
+    def rows(self, s, core, start, count):
+        first = core * HALF + start * PIECE
+        return self.w.at[s, pl.ds(pl.multiple_of(first, PIECE), count * PIECE)]
+
+    def mine(self, s, start, count):
+        return self.rows(s, self.here.core, start, count)
+
+    def first_parts(self, s, mode, lo):
+        if mode == DIRECT:
+            return [self.mine(s, 0, 4)]
+        if mode == PAIR:
+            return [self.mine(s, 2 * lo, 2)]
+        if mode == RING:
+            return [self.mine(s, self.here.y, 1)]
+        return [self.mine(s, self.here.y, 1), self.mine(s, (self.here.y + 2) % 4, 1)]
 
     def firsts(self):
-        for slot, (dz, dh) in enumerate([(1, 0), (3, 0), (0, 1), (2, 0), (1, 1), (3, 1), (2, 1)]):
-            if by_pair(dz, dh):
-                part = self.pair_part(self.own, self.here.lo)
-            else:
-                part = self.ring_part(self.own, self.here.y)
+        sends = [[], []]
+        for dz, dh in ORDER:
+            lo = (self.here.lo + dh) % 2
+            for n, part in enumerate(self.first_parts(self.own, MODES[dz, dh], lo)):
+                sends[n].append((n, part, self.here.at(dz=dz, hi=dh, lo=dh)))
+        for slot, (n, part, device) in enumerate(sends[0] + sends[1]):
             yield remote(
-                part,
-                part,
-                self.first_send.at[slot],
-                self.first_recv.at[self.own],
-                self.here.at(dz=dz, hi=dh, lo=dh),
+                part, part, self.first_send.at[slot], self.first_recv.at[self.own, n], device
             )
 
     def start(self):
         for copy in self.firsts():
             copy.start()
 
-    def paired(self, s):
+    def by_mode(self, s, act):
         dz = (self.here.z + 4 - s // 2) % 4
         dh = (self.here.hi + s) % 2
-        return dh, ((1 - dh) * (dz % 2) + dh * ((dz + 3) // 4 * -1 + 1)) == 1
+        for mode in range(4):
+            hits = [key for key, value in MODES.items() if value == mode]
+            if hits:
+                cond = (dz == hits[0][0]) & (dh == hits[0][1])
+                for key in hits[1:]:
+                    cond = cond | ((dz == key[0]) & (dh == key[1]))
+
+                @pl.when(cond)
+                def _():
+                    act(mode)
+
+    def wait(self, part, receive):
+        remote(part, part, self.first_send.at[0], receive, self.here.at()).wait_recv()
+
+    def relays(self, s, mode):
+        here = self.here
+        if mode == PAIR:
+            hops = [(here.at(lo=1), self.mine(s, 2 * here.lo, 2), self.mine(s, 2 - 2 * here.lo, 2))]
+        elif mode == DIRECT:
+            hops = []
+        else:
+            hops = [
+                (here.at(dy=k), self.mine(s, here.y, 1), self.mine(s, (here.y + 4 - k) % 4, 1))
+                for k in ((1, 3, 2) if mode == RING else (1, 3))
+            ]
+        for n, (device, part, back) in enumerate(hops):
+            yield (
+                remote(part, part, self.relay_send.at[s, n], self.relay_recv.at[s, n], device),
+                back,
+                self.relay_recv.at[s, n],
+            )
 
     def relay(self, s):
-        here = self.here
-        dh, paired = self.paired(s)
-
-        @pl.when(paired)
-        def _():
-            part = self.pair_part(s, (here.lo + dh) % 2)
-            remote(part, part, self.first_send.at[0], self.first_recv.at[s], here.at()).wait_recv()
-            self.pair_copy(s, dh).start()
-
-        @pl.when(jnp.logical_not(paired))
-        def _():
-            part = self.ring_part(s, here.y)
-            remote(part, part, self.first_send.at[0], self.first_recv.at[s], here.at()).wait_recv()
-            for k in (1, 3, 2):
-                self.ring_copy(s, k).start()
-
-    def pair_copy(self, s, dh):
-        part = self.pair_part(s, (self.here.lo + dh) % 2)
-        return remote(
-            part, part, self.pair_sem.at[0, s], self.pair_sem.at[1, s], self.here.at(lo=1)
-        )
-
-    def ring_copy(self, s, k):
-        part = self.ring_part(s, self.here.y)
-        return remote(
-            part, part, self.ring_send.at[s, k - 1], self.ring_recv.at[s, k - 1], self.here.at(dy=k)
-        )
+        def act(mode):
+            if mode != DIRECT:
+                self.wait(self.first_parts(s, mode, self.here.lo)[0], self.first_recv.at[s, 0])
+            for copy, _, _ in self.relays(s, mode):
+                copy.start()
+
+        self.by_mode(s, act)
 
     def core_copy(self, s):
-        part = self.half(s, self.here.core)
+        part = self.mine(s, 0, 4)
         return remote(
             part, part, self.core_sem.at[0, s], self.core_sem.at[1, s], self.here.at(core=1)
         )
 
     def swap(self, s):
-        here = self.here
-        dh, paired = self.paired(s)
-
-        @pl.when(paired)
-        def _():
-            part = self.pair_part(s, (here.lo + dh + 1) % 2)
-            remote(
-                part, part, self.pair_sem.at[0, s], self.pair_sem.at[1, s], here.at(lo=1)
-            ).wait_recv()
-
-        @pl.when(jnp.logical_not(paired))
-        def _():
-            for k in (1, 3, 2):
-                part = self.ring_part(s, (here.y + 4 - k) % 4)
-                remote(
-                    part,
-                    part,
-                    self.ring_send.at[s, k - 1],
-                    self.ring_recv.at[s, k - 1],
-                    here.at(dy=k),
-                ).wait_recv()
-
+        def act(mode):
+            for n, part in enumerate(self.first_parts(s, mode, self.here.lo)):
+                if n > 0 or mode == DIRECT:
+                    self.wait(part, self.first_recv.at[s, n])
+            for _, part, receive in self.relays(s, mode):
+                self.wait(part, receive)
+
+        self.by_mode(s, act)
         self.core_copy(s).start()
 
     def arrive(self, s):
-        part = self.half(s, 1 - self.here.core)
-        remote(
-            part, part, self.core_sem.at[0, s], self.core_sem.at[1, s], self.here.at(core=1)
-        ).wait_recv()
+        self.wait(self.rows(s, 1 - self.here.core, 0, 4), self.core_sem.at[1, s])
 
     def finish(self):
         for copy in self.firsts():
@@ -329,17 +334,11 @@
         def each(s, _):
             @pl.when(s != self.own)
             def _():
-                dh, paired = self.paired(s)
-
-                @pl.when(paired)
-                def _():
-                    self.pair_copy(s, dh).wait_send()
-
-                @pl.when(jnp.logical_not(paired))
-                def _():
-                    for k in (1, 3, 2):
-                        self.ring_copy(s, k).wait_send()
-
+                def act(mode):
+                    for copy, _, _ in self.relays(s, mode):
+                        copy.wait_send()
+
+                self.by_mode(s, act)
                 self.core_copy(s).wait_send()
 
             return 0
@@ -513,9 +512,8 @@
     load_sem,
     first_send,
     first_recv,
-    pair_sem,
-    ring_send,
-    ring_recv,
+    relay_send,
+    relay_recv,
     core_sem,
     sum_core,
     sum_ring_send,
@@ -527,7 +525,7 @@
     renew_core,
 ):
     here = Place()
-    gather = Gather(here, w, first_send, first_recv, pair_sem, ring_send, ring_recv, core_sem)
+    gather = Gather(here, w, first_send, first_recv, relay_send, relay_recv, core_sem)
     exchange = Exchange(
         here,
         total,
@@ -560,18 +558,22 @@
     own_rows.wait()
     renewal.compute(rows, moment, second, stale, new_moment, new_second)
 
+    def passing(s, _):
+        @pl.when(s != gather.own)
+        def _():
+            gather.relay(s)
+
+        return 0
+
+    lax.fori_loop(0, SECTIONS, passing, 0)
+    renewal.to_ring()
+
     def forward(tick, _):
         @pl.when((tick < SECTIONS) & (tick != gather.own))
         def _():
-            gather.relay(tick)
-
-        later = tick - 1
-
-        @pl.when((later >= 0) & (later < SECTIONS) & (later != gather.own))
-        def _():
-            gather.swap(later)
-
-        s = tick - 2
+            gather.swap(tick)
+
+        s = tick - 1
 
         @pl.when(s >= 0)
         def _():
@@ -583,8 +585,8 @@
 
         return 0
 
-    lax.fori_loop(0, SECTIONS + 2, forward, 0)
-    renewal.to_ring()
+    lax.fori_loop(0, SECTIONS + 1, forward, 0)
+    renewal.to_pair()
 
     def backward(i, _):
         s = SECTIONS - 1 - i
@@ -602,19 +604,11 @@
             weight_grad(s, taps, back, put)
             exchange.to_core(s % 2)
 
-        @pl.when(s == 2 * here.z)
-        def _():
-            exchange.to_cross(1)
-
         @pl.when(s > 0)
         def _():
             input_grad(s, w, back, upstream)
 
-        @pl.when(s == 5)
-        def _():
-            renewal.to_pair()
-
-        @pl.when(s == 3)
+        @pl.when(s == 1)
         def _():
             renewal.to_core()
 
@@ -625,6 +619,7 @@
     store = pltpu.make_async_copy(fresh, new_weights, load_sem.at[0])
     store.start()
     exchange.to_ring(0)
+    exchange.to_cross(1)
     exchange.to_cross(0)
     exchange.finish(grads)
     renewal.finish()
@@ -653,8 +648,8 @@
         out_specs=(vmem, vmem, vmem, away),
         scratch_shapes=[
             pltpu.VMEM((SECTIONS, ROWS, CHAN), BF16),
-            pltpu.VMEM((SECTIONS, FRAMES + 2, WIDTH + 2, HEIGHT, 3 * CHAN), BF16),
-            pltpu.VMEM((FRAMES + 2, WIDTH + 2, HEIGHT, 3 * CHAN), BF16),
+            pltpu.VMEM((SECTIONS, FRAMES, WIDTH + 2, HEIGHT, 3 * CHAN), BF16),
+            pltpu.VMEM((FRAMES, WIDTH + 2, HEIGHT, 3 * CHAN), BF16),
             pltpu.VMEM((SECTIONS, CELLS, CHAN), F32),
             pltpu.VMEM((CELLS, CHAN), F32),
             pltpu.VMEM((SHARD, CHAN), BF16),
@@ -667,9 +662,8 @@
             pltpu.VMEM((2, 2, SHARD, CHAN), BF16),
             pltpu.VMEM((3, SHARD, CHAN), BF16),
             dma((2,)),
-            dma((7,)),
-            dma((SECTIONS,)),
-            dma((2, SECTIONS)),
+            dma((14,)),
+            dma((SECTIONS, 2)),
             dma((SECTIONS, 3)),
             dma((SECTIONS, 3)),
             dma((2, SECTIONS)),

time: 93.5 us -> 74.5 us (0.80)
  Pallas kernels: 86.4 us -> 68.2 us
    pallas_call x1, Pallas kernels: 86.4 us -> 68.2 us  [window(): pl.pallas_call(window_kernel, out_shape=(shard, shard, shard, jax.ShapeDt...]
where the time goes in v4:
time: 74.5 us; the launch traced here: 74.1 us
  Pallas kernels  68.2 us (92%)
  local copies, waits for them, and re-layouts  5.3 us (7%)
    pallas_call x1, Pallas kernels, window(): pl.pallas_call(window_kernel, out_shape=(shard, shard, shard, jax.ShapeDt...  68.2 us
    unnamed x8, local copies, waits for them, and re-layouts  5.3 us

profile of v4, /device:TPU:1, one launch (start us, length us, event | category | flops | bytes accessed | tf_op | source)
XLA Modules:
  0.0 74.1 jit_solution(1532389169858183207)
XLA Ops:
  0.6 68.2 %shard_map.102 = (f32[216,128]{1,0:T(8,128)}, f32[216,128]{1,0:T(8,128)}, f32[216,128]{1,0:T(8,128)}, bf16[2,4,2,216,128]{4,3,2,1,0:T(8,128)(2,1)}) custom-call(s32[2,2]{1,0:T(2,128)} %offsets.1, bf16[2,4,384,128]{3,2,1,0:T(8,128)(2,1)} %bitcast.14, bf16[3456,128]{1,0:T(8,128)(2,1)} %bitcast.11, bf16[16,216,128]{2,1,0:T(8,128)(2,1)} %bitcast.12, ...), custom_call_target="tpu_custom_call" | custom-call | tf_op jit(solution)/shard_map/pallas_call | solution.py:635
  68.8 0.0 copy-start.1
  68.8 1.6 %copy.15 = f32[1,216,128]{2,1,0:T(8,128)} copy(f32[1,216,128]{2,1,0:T(8,128)} %bitcast.18) | data formatting | bytes 221184
  70.4 0.0 copy-done.1
  70.4 0.0 copy-start
  70.4 0.6 copy.16
  71.1 0.3 copy-done
  71.3 0.6 copy.17
  72.0 2.1 %copy.18 = bf16[1,3456,128]{2,1,0:T(8,128)(2,1)} copy(bf16[1,3456,128]{2,1,0:T(8,128)(2,1)} %bitcast.13) | data formatting | bytes 1769472
Async XLA Ops:
  68.8 1.6 %copy-start.1 = (f32[216,128]{1,0:T(8,128)S(1)}, f32[216,128]{1,0:T(8,128)}, u32[]{:S(2)}) copy-start(f32[216,128]{1,0:T(8,128)} %get-tuple-element.9) | copy-start | bytes 331780
  70.4 0.9 %copy-start = (f32[216,128]{1,0:T(8,128)S(1)}, f32[216,128]{1,0:T(8,128)}, u32[]{:S(2)}) copy-start(f32[216,128]{1,0:T(8,128)} %get-tuple-element.10) | copy-start | bytes 331780

commit v5 on v4

--- a/solution.py
+++ b/solution.py
@@ -431,17 +431,20 @@
             self.cross_copy(0, slot).wait_send()
 
 
+def moments(moment, second, stale):
+    first = beta_one * moment + (1.0 - beta_one) * stale
+    square = beta_two * second + (1.0 - beta_two) * stale * stale
+    return first, square
+
+
 class Renewal:
     def __init__(self, here, fresh, ring_sem, pair_sem, core_sem):
         self.here, self.fresh = here, fresh
         self.ring_sem, self.pair_sem, self.core_sem = ring_sem, pair_sem, core_sem
 
-    def compute(self, rows, moment, second, stale, new_moment, new_second):
+    def compute(self, rows, moment, second, stale):
         here = self.here
-        first = beta_one * moment[...] + (1.0 - beta_one) * stale[...]
-        square = beta_two * second[...] + (1.0 - beta_two) * stale[...] * stale[...]
-        new_moment[...] = first
-        new_second[...] = square
+        first, square = moments(moment[...], second[...], stale[...])
         step = learn_rate * first / (jnp.sqrt(square) + adam_eps)
         self.fresh[here.lo, here.y, here.core] = (rows[...].astype(F32) - step).astype(BF16)
 
@@ -492,8 +495,6 @@
     stale,
     cotangent,
     grads,
-    new_moment,
-    new_second,
     new_weights,
     w,
     taps,
@@ -501,6 +502,9 @@
     slope,
     upstream,
     rows,
+    clip,
+    given,
+    old,
     fresh,
     total,
     give,
@@ -540,23 +544,35 @@
     renewal = Renewal(here, fresh, renew_ring, renew_pair, renew_core)
     load = pltpu.make_async_copy(weights, w.at[gather.own], load_sem.at[0])
     load.start()
-    own_rows = pltpu.make_async_copy(
-        shards16.at[here.lo * 8 + here.y * 2 + here.core], rows, load_sem.at[1]
-    )
-    own_rows.start()
+    loads = [
+        pltpu.make_async_copy(source, place, load_sem.at[n + 1])
+        for n, (source, place) in enumerate(
+            (
+                (clips.at[here.hi], clip),
+                (cotangent.at[here.hi], given),
+                (shards16.at[here.lo * 8 + here.y * 2 + here.core], rows),
+                (moment, old.at[0]),
+                (second, old.at[1]),
+                (stale, old.at[2]),
+            )
+        )
+    ]
     barrier = pltpu.get_barrier_semaphore()
     partners = here.partners()
     for partner in partners:
         pl.semaphore_signal(barrier, inc=1, device_id=partner, device_id_type=MESH_ID)
+    for other in loads:
+        other.start()
     load.wait()
     pl.semaphore_wait(barrier, len(partners))
     gather.start()
 
     clear_edges(taps, back)
-    crop(clips.at[here.hi], offsets[here.hi, 0], offsets[here.hi, 1], taps)
-    reorder(cotangent.at[here.hi], upstream)
-    own_rows.wait()
-    renewal.compute(rows, moment, second, stale, new_moment, new_second)
+    for other in loads:
+        other.wait()
+    crop(clip, offsets[here.hi, 0], offsets[here.hi, 1], taps)
+    reorder(given, upstream)
+    renewal.compute(rows, old.at[0], old.at[1], old.at[2])
 
     def passing(s, _):
         @pl.when(s != gather.own)
@@ -634,18 +650,9 @@
     shard = jax.ShapeDtypeStruct((SHARD, CHAN), F32)
     return pl.pallas_call(
         window_kernel,
-        out_shape=(shard, shard, shard, jax.ShapeDtypeStruct((2, 4, 2, SHARD, CHAN), BF16)),
-        in_specs=[
-            pl.BlockSpec(memory_space=pltpu.SMEM),
-            vmem,
-            away,
-            away,
-            vmem,
-            vmem,
-            vmem,
-            vmem,
-        ],
-        out_specs=(vmem, vmem, vmem, away),
+        out_shape=(shard, jax.ShapeDtypeStruct((2, 4, 2, SHARD, CHAN), BF16)),
+        in_specs=[pl.BlockSpec(memory_space=pltpu.SMEM)] + [away] * 7,
+        out_specs=(vmem, away),
         scratch_shapes=[
             pltpu.VMEM((SECTIONS, ROWS, CHAN), BF16),
             pltpu.VMEM((SECTIONS, FRAMES, WIDTH + 2, HEIGHT, 3 * CHAN), BF16),
@@ -653,6 +660,9 @@
             pltpu.VMEM((SECTIONS, CELLS, CHAN), F32),
             pltpu.VMEM((CELLS, CHAN), F32),
             pltpu.VMEM((SHARD, CHAN), BF16),
+            pltpu.VMEM(clips.shape[1:], BF16),
+            pltpu.VMEM(cotangent.shape[1:], BF16),
+            pltpu.VMEM((3, SHARD, CHAN), F32),
             pltpu.VMEM((2, 4, 2, SHARD, CHAN), BF16),
             pltpu.VMEM((2, ROWS, CHAN), F32),
             pltpu.VMEM((2, 8, SHARD, CHAN), BF16),
@@ -661,7 +671,7 @@
             pltpu.VMEM((2, 3, 2, SHARD, CHAN), BF16),
             pltpu.VMEM((2, 2, SHARD, CHAN), BF16),
             pltpu.VMEM((3, SHARD, CHAN), BF16),
-            dma((2,)),
+            dma((7,)),
             dma((14,)),
             dma((SECTIONS, 2)),
             dma((SECTIONS, 3)),
@@ -691,9 +701,60 @@
     )
 
 
+def finish_kernel(
+    summed, moment, second, stale, gathered, grads, new_moment, new_second, new_weights, *scratch
+):
+    own, m, v, g, room, load_sem, store_sem = scratch
+    places = (room, own, g, m, v)
+    loads = [
+        pltpu.make_async_copy(source, place, load_sem.at[n])
+        for n, (source, place) in enumerate(
+            zip((gathered, summed, stale, moment, second), places)
+        )
+    ]
+    stores = [
+        pltpu.make_async_copy(place, target, store_sem.at[n])
+        for n, (place, target) in enumerate(
+            zip((room, own, m, v), (new_weights, grads, new_moment, new_second))
+        )
+    ]
+    for load in loads:
+        load.start()
+    for n in range(2):
+        loads[n].wait()
+        stores[n].start()
+    for load in loads[2:]:
+        load.wait()
+    first, square = moments(m[...], v[...], g[...])
+    m[...] = first
+    v[...] = square
+    for store in stores[2:]:
+        store.start()
+    for store in stores:
+        store.wait()
+
+
+def finish(summed, moment, second, stale, gathered):
+    away = pl.BlockSpec(memory_space=pl.ANY)
+    shard = jax.ShapeDtypeStruct((SHARD, CHAN), F32)
+    return pl.pallas_call(
+        finish_kernel,
+        out_shape=(shard, shard, shard, jax.ShapeDtypeStruct(gathered.shape, BF16)),
+        in_specs=[away] * 5,
+        out_specs=(away,) * 4,
+        scratch_shapes=[pltpu.VMEM((SHARD, CHAN), F32)] * 4
+        + [
+            pltpu.VMEM(gathered.shape, BF16),
+            pltpu.SemaphoreType.DMA((5,)),
+            pltpu.SemaphoreType.DMA((4,)),
+        ],
+        compiler_params=pltpu.CompilerParams(vmem_limit_bytes=56 << 20),
+    )(summed, moment, second, stale, gathered)
+
+
 def shards(clips, offsets, weights, moment, second, stale_grads, cotangent):
     micro = clips.shape[0]
-    grads, first_new, second_new, fresh = window(
+    summed, fresh = window(
         offsets,
         clips.reshape(micro, FRAMES, -1, CHAN),
         weights[0],
@@ -701,6 +762,9 @@
         second[0],
         stale_grads[0],
         cotangent.reshape(micro, FRAMES, PLANE, CHAN),
+    )
+    grads, first_new, second_new, fresh = finish(
+        summed, moment[0], second[0], stale_grads[0], fresh
     )
     return (grads[None], first_new[None], second_new[None], fresh.reshape(1, ROWS, CHAN))
 

time: 74.5 us -> 70.7 us (0.949)
  local copies, waits for them, and re-layouts: 5.3 us -> 0 us
  Pallas kernels: 68.2 us -> 69.8 us
    unnamed x8 -> x0, local copies, waits for them, and re-layouts: 5.3 us -> none
    pallas_call x1 -> x2, Pallas kernels: 68.2 us -> 69.8 us  [the longest x1 67.5 us: window(): pl.pallas_call(window_kernel, out_shape=(shard, jax.ShapeDtypeStruct((2,...]
where the time goes in v5:
time: 70.7 us; the launch traced here: 70.4 us
  Pallas kernels  69.8 us (99%)
    pallas_call x1, Pallas kernels, window(): pl.pallas_call(window_kernel, out_shape=(shard, jax.ShapeDtypeStruct((2,...  67.5 us
    pallas_call x1, Pallas kernels, finish(): pl.pallas_call(finish_kernel, out_shape=(shard, shard, shard, jax.ShapeDt...  2.26 us

profile of v5, /device:TPU:1, one launch (start us, length us, event | category | flops | bytes accessed | tf_op | source)
XLA Modules:
  0.0 70.4 jit_solution(11878908367155413821)
XLA Ops:
  0.6 67.5 %shard_map.102 = (f32[216,128]{1,0:T(8,128)}, bf16[2,4,2,216,128]{4,3,2,1,0:T(8,128)(2,1)}) custom-call(s32[2,2]{1,0:T(2,128)} %offsets.1, bf16[2,4,384,128]{3,2,1,0:T(8,128)(2,1)} %bitcast.13, bf16[3456,128]{1,0:T(8,128)(2,1)} %bitcast.11, bf16[16,216,128]{2,1,0:T(8,128)(2,1)} %bitcast.12, f32[216,128]{1,0:T(8,128)} %bitcast.14, f32[216,128]{1,0:T(8,128)} %bitcast.16, ...), custom_call_target="tpu_custom_call" | custom-call | tf_op jit(solution)/shard_map/pallas_call | solution.py:651
  68.1 2.3 %shard_map.103 = (f32[216,128]{1,0:T(8,128)}, f32[216,128]{1,0:T(8,128)}, f32[216,128]{1,0:T(8,128)}, bf16[2,4,2,216,128]{4,3,2,1,0:T(8,128)(2,1)}) custom-call(f32[216,128]{1,0:T(8,128)} %get-tuple-element.10.summed, f32[216,128]{1,0:T(8,128)} %bitcast.15, f32[216,128]{1,0:T(8,128)} %bitcast.17, f32[216,128]{1,0:T(8,128)} %bitcast.19, ...), custom_call_target="tpu_custom_call" | custom-call | tf_op jit(solution)/shard_map/pallas_call | solution.py:740

commit v6 on v5

--- a/solution.py
+++ b/solution.py
@@ -100,7 +100,7 @@
     store_shifted(store, delta)
 
 
-def weight_grad(s, taps, back, put):
+def weight_grad(s, taps, back, put, done):
     field = taps[s, :, 1 : 1 + WIDTH, :, CHAN : 2 * CHAN].reshape(CELLS, CHAN)
     turned = field.astype(F32).T.astype(BF16)
     for a in range(3):
@@ -120,6 +120,8 @@
             for b in range(3):
                 first = (c * 3 + 2 - b) * CHAN
                 put((a * 3 + b) * 3 + c, out[:, first : first + CHAN])
+        if a > 0:
+            done(a - 1)
 
 
 def input_grad(s, w, back, upstream):
@@ -212,16 +214,9 @@
 
 
 DIRECT, PAIR, RING, NEAR = range(4)
-MODES = {
-    (1, 0): DIRECT,
-    (3, 0): DIRECT,
-    (2, 0): NEAR,
-    (0, 1): PAIR,
-    (1, 1): RING,
-    (3, 1): RING,
-    (2, 1): NEAR,
-}
+MODES = {(1, 0): DIRECT, (3, 0): DIRECT, (2, 0): NEAR, (0, 1): PAIR, (1, 1): RING, (3, 1): RING, (2, 1): RING}
 ORDER = ((2, 0), (2, 1), (1, 0), (3, 0), (0, 1), (1, 1), (3, 1))
+RELAYS = ((0, 1), (1, 1), (3, 1), (2, 1), (2, 0), (1, 0), (3, 0))
 
 
 class Gather:
@@ -248,20 +243,28 @@
             return [self.mine(s, self.here.y, 1)]
         return [self.mine(s, self.here.y, 1), self.mine(s, (self.here.y + 2) % 4, 1)]
 
-    def firsts(self):
-        sends = [[], []]
-        for dz, dh in ORDER:
-            lo = (self.here.lo + dh) % 2
-            for n, part in enumerate(self.first_parts(self.own, MODES[dz, dh], lo)):
-                sends[n].append((n, part, self.here.at(dz=dz, hi=dh, lo=dh)))
-        for slot, (n, part, device) in enumerate(sends[0] + sends[1]):
+    def firsts(self, dz, dh):
+        lo = (self.here.lo + dh) % 2
+        slot = 2 * ORDER.index((dz, dh))
+        for n, part in enumerate(self.first_parts(self.own, MODES[dz, dh], lo)):
             yield remote(
-                part, part, self.first_send.at[slot], self.first_recv.at[self.own, n], device
+                part,
+                part,
+                self.first_send.at[slot + n],
+                self.first_recv.at[self.own, n],
+                self.here.at(dz=dz, hi=dh, lo=dh),
             )
 
     def start(self):
-        for copy in self.firsts():
-            copy.start()
+        for z in range(4):
+
+            @pl.when(self.here.z == z)
+            def _():
+                for target, dh in ((0, 1), (2, 1), (1, 1), (3, 1), (0, 0), (2, 0), (1, 0), (3, 0)):
+                    dz = (target - z) % 4
+                    if (dz, dh) != (0, 0):
+                        for copy in self.firsts(dz, dh):
+                            copy.start()
 
     def by_mode(self, s, act):
         dz = (self.here.z + 4 - s // 2) % 4
@@ -298,14 +301,11 @@
                 self.relay_recv.at[s, n],
             )
 
-    def relay(self, s):
-        def act(mode):
-            if mode != DIRECT:
-                self.wait(self.first_parts(s, mode, self.here.lo)[0], self.first_recv.at[s, 0])
-            for copy, _, _ in self.relays(s, mode):
-                copy.start()
-
-        self.by_mode(s, act)
+    def relay(self, s, mode):
+        if mode != DIRECT:
+            self.wait(self.first_parts(s, mode, self.here.lo)[0], self.first_recv.at[s, 0])
+        for copy, _, _ in self.relays(s, mode):
+            copy.start()
 
     def core_copy(self, s):
         part = self.mine(s, 0, 4)
@@ -328,8 +328,9 @@
         self.wait(self.rows(s, 1 - self.here.core, 0, 4), self.core_sem.at[1, s])
 
     def finish(self):
-        for copy in self.firsts():
-            copy.wait_send()
+        for dz, dh in ORDER:
+            for copy in self.firsts(dz, dh):
+                copy.wait_send()
 
         def each(s, _):
             @pl.when(s != self.own)
@@ -357,36 +358,36 @@
         start = pl.multiple_of((2 * j + core) * SHARD, 8)
         return self.total[i, pl.ds(start, SHARD)]
 
-    def core_copy(self, i):
+    def core_copy(self, i, lo):
         return remote(
-            self.give.at[i],
-            self.taken.at[i],
-            self.core_sem.at[0, i],
-            self.core_sem.at[1, i],
+            self.give.at[i, lo],
+            self.taken.at[i, lo],
+            self.core_sem.at[0, i, lo],
+            self.core_sem.at[1, i, lo],
             self.here.at(core=1),
         )
 
-    def to_core(self, i):
-        for j in range(8):
-            self.give[i, j] = self.shard(i, j, 1 - self.here.core).astype(BF16)
-        self.core_copy(i).start()
-
-    def ring_copy(self, i, k):
+    def to_core(self, i, lo):
+        for y in range(4):
+            self.give[i, lo, y] = self.shard(i, lo * 4 + y, 1 - self.here.core).astype(BF16)
+        self.core_copy(i, lo).start()
+
+    def ring_copy(self, i, lo, k):
         return remote(
-            self.summed.at[i, :, (self.here.y + k) % 4],
-            self.ring.at[i, k - 1],
-            self.ring_send.at[i, k - 1],
-            self.ring_recv.at[i, k - 1],
+            self.summed.at[i, lo, (self.here.y + k) % 4],
+            self.ring.at[i, lo, k - 1],
+            self.ring_send.at[i, lo, k - 1],
+            self.ring_recv.at[i, lo, k - 1],
             self.here.at(dy=k),
         )
 
-    def to_ring(self, i):
-        self.core_copy(i).wait_recv()
-        for j in range(8):
-            both = self.shard(i, j, self.here.core) + self.taken[i, j].astype(F32)
-            self.summed[i, j // 4, j % 4] = both.astype(BF16)
+    def to_ring(self, i, lo):
+        self.core_copy(i, lo).wait_recv()
+        for y in range(4):
+            both = self.shard(i, lo * 4 + y, self.here.core) + self.taken[i, lo, y].astype(F32)
+            self.summed[i, lo, y] = both.astype(BF16)
         for k in (2, 1, 3):
-            self.ring_copy(i, k).start()
+            self.ring_copy(i, lo, k).start()
 
     def cross_copy(self, i, slot):
         hi, lo = ((0, 1), (1, 0), (1, 1))[slot]
@@ -398,23 +399,31 @@
             self.here.at(hi=hi, lo=lo),
         )
 
-    def to_cross(self, i):
+    def to_cross(self, i, lo):
+        here = self.here
         for k in (1, 3, 2):
-            self.ring_copy(i, k).wait_recv()
-        for lo in range(2):
-            value = self.summed[i, lo, self.here.y].astype(F32)
-            for k in range(3):
-                value = value + self.ring[i, k, lo].astype(F32)
-            self.kept[i, lo] = value.astype(BF16)
-
-        @pl.when(self.here.hi == i)
+            self.ring_copy(i, lo, k).wait_recv()
+        value = self.summed[i, lo, here.y].astype(F32)
+        for k in range(3):
+            value = value + self.ring[i, lo, k].astype(F32)
+        self.kept[i, lo] = value.astype(BF16)
+
+        @pl.when((here.hi == i) & (here.lo != lo))
         def _():
             self.cross_copy(i, 0).start()
 
-        @pl.when(self.here.hi != i)
+        @pl.when((here.hi != i) & (here.lo == lo))
         def _():
             self.cross_copy(i, 1).start()
+
+        @pl.when((here.hi != i) & (here.lo != lo))
+        def _():
             self.cross_copy(i, 2).start()
+
+    def across(self):
+        for i in (1, 0):
+            for lo in range(2):
+                self.to_cross(i, lo)
 
     def finish(self, grads):
         for slot in range(3):
@@ -424,9 +433,10 @@
             value = value + self.crossed[slot].astype(F32)
         grads[...] = value
         for i in range(2):
-            self.core_copy(i).wait_send()
-            for k in (1, 2, 3):
-                self.ring_copy(i, k).wait_send()
+            for lo in range(2):
+                self.core_copy(i, lo).wait_send()
+                for k in (1, 2, 3):
+                    self.ring_copy(i, lo, k).wait_send()
         for slot in range(3):
             self.cross_copy(0, slot).wait_send()
 
@@ -574,14 +584,8 @@
     reorder(given, upstream)
     renewal.compute(rows, old.at[0], old.at[1], old.at[2])
 
-    def passing(s, _):
-        @pl.when(s != gather.own)
-        def _():
-            gather.relay(s)
-
-        return 0
-
-    lax.fori_loop(0, SECTIONS, passing, 0)
+    for dz, dh in RELAYS:
+        gather.relay((here.z + 4 - dz) % 4 * 2 + (here.hi + dh) % 2, MODES[dz, dh])
     renewal.to_ring()
 
     def forward(tick, _):
@@ -603,40 +607,38 @@
 
     lax.fori_loop(0, SECTIONS + 1, forward, 0)
     renewal.to_pair()
+    last = 2 * here.z
 
     def backward(i, _):
         s = SECTIONS - 1 - i
         shifted_delta(s, upstream, slope, back)
 
-        @pl.when(s == 2 * here.z)
+        @pl.when(s == last)
         def _():
-            exchange.to_ring(1)
-
-        @pl.when(s // 2 == here.z)
+            exchange.to_ring(1, 0)
+            exchange.to_ring(1, 1)
+
+        @pl.when(s < last + 2)
         def _():
             def put(tap, block):
                 total[s % 2, tap * CHAN : (tap + 1) * CHAN] = block
 
-            weight_grad(s, taps, back, put)
-            exchange.to_core(s % 2)
-
-        @pl.when(s > 0)
+            weight_grad(s, taps, back, put, lambda lo: exchange.to_core(s % 2, lo))
+
+        @pl.when(s > last)
         def _():
             input_grad(s, w, back, upstream)
 
-        @pl.when(s == 1)
-        def _():
-            renewal.to_core()
-
         return 0
 
-    lax.fori_loop(0, SECTIONS, backward, 0)
+    lax.fori_loop(0, SECTIONS - last, backward, 0)
+    exchange.to_ring(0, 0)
+    exchange.to_ring(0, 1)
+    renewal.to_core()
+    exchange.across()
     renewal.arrive()
     store = pltpu.make_async_copy(fresh, new_weights, load_sem.at[0])
     store.start()
-    exchange.to_ring(0)
-    exchange.to_cross(1)
-    exchange.to_cross(0)
     exchange.finish(grads)
     renewal.finish()
     gather.finish()
@@ -665,10 +667,10 @@
             pltpu.VMEM((3, SHARD, CHAN), F32),
             pltpu.VMEM((2, 4, 2, SHARD, CHAN), BF16),
             pltpu.VMEM((2, ROWS, CHAN), F32),
-            pltpu.VMEM((2, 8, SHARD, CHAN), BF16),
-            pltpu.VMEM((2, 8, SHARD, CHAN), BF16),
             pltpu.VMEM((2, 2, 4, SHARD, CHAN), BF16),
-            pltpu.VMEM((2, 3, 2, SHARD, CHAN), BF16),
+            pltpu.VMEM((2, 2, 4, SHARD, CHAN), BF16),
+            pltpu.VMEM((2, 2, 4, SHARD, CHAN), BF16),
+            pltpu.VMEM((2, 2, 3, SHARD, CHAN), BF16),
             pltpu.VMEM((2, 2, SHARD, CHAN), BF16),
             pltpu.VMEM((3, SHARD, CHAN), BF16),
             dma((7,)),
@@ -677,9 +679,9 @@
             dma((SECTIONS, 3)),
             dma((SECTIONS, 3)),
             dma((2, SECTIONS)),
-            dma((2, 2)),
-            dma((2, 3)),
-            dma((2, 3)),
+            dma((2, 2, 2)),
+            dma((2, 2, 3)),
+            dma((2, 2, 3)),
             dma((3,)),
             dma((3,)),
             dma((2, 3)),

time: 70.7 us -> 67.9 us (0.960)
  the two profiles are of different devices: /device:TPU:1 before, /device:TPU:98 now
where the time goes in v6:
time: 67.9 us; the launch traced here: 67.7 us
  Pallas kernels  67.1 us (99%)
    pallas_call x1, Pallas kernels, window(): pl.pallas_call(window_kernel, out_shape=(shard, jax.ShapeDtypeStruct((2,...  64.8 us
    pallas_call x1, Pallas kernels, finish(): pl.pallas_call(finish_kernel, out_shape=(shard, shard, shard, jax.ShapeDt...  2.26 us

profile of v6, /device:TPU:98, one launch (start us, length us, event | category | flops | bytes accessed | tf_op | source)
XLA Modules:
  0.0 67.7 jit_solution(12218337902589589659)
XLA Ops:
  0.6 64.8 %shard_map.102 = (f32[216,128]{1,0:T(8,128)}, bf16[2,4,2,216,128]{4,3,2,1,0:T(8,128)(2,1)}) custom-call(s32[2,2]{1,0:T(2,128)} %offsets.1, bf16[2,4,384,128]{3,2,1,0:T(8,128)(2,1)} %bitcast.13, bf16[3456,128]{1,0:T(8,128)(2,1)} %bitcast.11, bf16[16,216,128]{2,1,0:T(8,128)(2,1)} %bitcast.12, f32[216,128]{1,0:T(8,128)} %bitcast.14, f32[216,128]{1,0:T(8,128)} %bitcast.16, ...), custom_call_target="tpu_custom_call" | custom-call | tf_op jit(solution)/shard_map/pallas_call | solution.py:653
  65.5 2.3 %shard_map.103 = (f32[216,128]{1,0:T(8,128)}, f32[216,128]{1,0:T(8,128)}, f32[216,128]{1,0:T(8,128)}, bf16[2,4,2,216,128]{4,3,2,1,0:T(8,128)(2,1)}) custom-call(f32[216,128]{1,0:T(8,128)} %get-tuple-element.10.summed, f32[216,128]{1,0:T(8,128)} %bitcast.15, f32[216,128]{1,0:T(8,128)} %bitcast.17, f32[216,128]{1,0:T(8,128)} %bitcast.19, ...), custom_call_target="tpu_custom_call" | custom-call | tf_op jit(solution)/shard_map/pallas_call | solution.py:742

commit v7 on v6

--- a/solution.py
+++ b/solution.py
@@ -66,7 +66,7 @@
     )
 
 
-def forward_section(s, w, taps, slope, last):
+def forward_section(s, w, taps, slope):
     field = taps[s].reshape(FRAMES * (WIDTH + 2) * HEIGHT, 3 * CHAN)
     lhs = field_columns(field)
     late = dot(lhs, tap_block(w, s, (1, 2), lambda b, c: (b, c), 0))
@@ -83,21 +83,17 @@
     sigma = jax.nn.sigmoid(pre)
     slope[s] = sigma * (1.0 + pre * (1.0 - sigma))
 
-    @pl.when(s < last)
-    def _():
-        def store(b, moved):
-            taps[s + 1, :, 1 : 1 + WIDTH, :, b * CHAN : (b + 1) * CHAN] = moved
-
-        store_shifted(store, pre * sigma)
-
-
-def shifted_delta(s, upstream, slope, back):
-    delta = upstream[...] * slope[s]
-
     def store(b, moved):
-        back[:, 1 : 1 + WIDTH, :, b * CHAN : (b + 1) * CHAN] = moved
-
-    store_shifted(store, delta)
+        taps[s + 1, :, 1 : 1 + WIDTH, :, b * CHAN : (b + 1) * CHAN] = moved
+
+    store_shifted(store, pre * sigma)
+
+
+def store_delta(s, upstream, slope, back):
+    def store(b, moved):
+        back[s % 2, :, 1 : 1 + WIDTH, :, b * CHAN : (b + 1) * CHAN] = moved
+
+    store_shifted(store, upstream * slope[s])
 
 
 def weight_grad(s, taps, back, put, done):
@@ -108,7 +104,7 @@
         lhs = turned[:, : frames * PLANE]
         rhs = jnp.concatenate(
             [
-                back[2 - a : 2 - a + frames, 2 - c : 2 - c + WIDTH].reshape(
+                back[s % 2, 2 - a : 2 - a + frames, 2 - c : 2 - c + WIDTH].reshape(
                     frames * PLANE, 3 * CHAN
                 )
                 for c in range(3)
@@ -124,8 +120,8 @@
             done(a - 1)
 
 
-def input_grad(s, w, back, upstream):
-    field = back[...].reshape(FRAMES * (WIDTH + 2) * HEIGHT, 3 * CHAN)
+def input_grad(s, w, back, slope):
+    field = back[s % 2].reshape(FRAMES * (WIDTH + 2) * HEIGHT, 3 * CHAN)
     lhs = field_columns(field)
     flip = lambda b, c: (2 - b, 2 - c)
     late = dot_turned(lhs, tap_block(w, s, (1, 2), flip, 1))
@@ -139,7 +135,7 @@
         ],
         axis=0,
     )
-    upstream[...] = total * SCALE
+    store_delta(s - 1, total * SCALE, slope, back)
 
 
 def crop(clip, offset_y, offset_x, taps):
@@ -173,8 +169,9 @@
         return 0
 
     lax.fori_loop(0, SECTIONS, wipe, 0)
-    back[:, 0] = edge
-    back[:, WIDTH + 1] = edge
+    for n in range(2):
+        back[n, :, 0] = edge
+        back[n, :, WIDTH + 1] = edge
 
 
 MESH_ID = pl.DeviceIdType.MESH
@@ -214,9 +211,10 @@
 
 
 DIRECT, PAIR, RING, NEAR = range(4)
-MODES = {(1, 0): DIRECT, (3, 0): DIRECT, (2, 0): NEAR, (0, 1): PAIR, (1, 1): RING, (3, 1): RING, (2, 1): RING}
+MODES = {(1, 0): DIRECT, (3, 0): DIRECT, (2, 0): NEAR, (0, 1): DIRECT, (1, 1): RING, (3, 1): RING, (2, 1): RING}
 ORDER = ((2, 0), (2, 1), (1, 0), (3, 0), (0, 1), (1, 1), (3, 1))
-RELAYS = ((0, 1), (1, 1), (3, 1), (2, 1), (2, 0), (1, 0), (3, 0))
+RELAYS = ((1, 1), (3, 1), (2, 1), (2, 0))
+SENDS = (((1, 1), (2, 1), (3, 1), (2, 0), (0, 1), (1, 0), (3, 0)), ((3, 1), (1, 1), (2, 1), (2, 0), (3, 0), (0, 1), (1, 0)), ((2, 1), (3, 1), (1, 1), (2, 0), (3, 0), (0, 1), (1, 0)), ((1, 1), (2, 1), (3, 1), (2, 0), (1, 0), (3, 0), (0, 1)))
 
 
 class Gather:
@@ -260,11 +258,9 @@
 
             @pl.when(self.here.z == z)
             def _():
-                for target, dh in ((0, 1), (2, 1), (1, 1), (3, 1), (0, 0), (2, 0), (1, 0), (3, 0)):
-                    dz = (target - z) % 4
-                    if (dz, dh) != (0, 0):
-                        for copy in self.firsts(dz, dh):
-                            copy.start()
+                for dz, dh in SENDS[z]:
+                    for copy in self.firsts(dz, dh):
+                        copy.start()
 
     def by_mode(self, s, act):
         dz = (self.here.z + 4 - s // 2) % 4
@@ -601,7 +597,7 @@
             def _():
                 gather.arrive(s)
 
-            forward_section(s, w, taps, slope, SECTIONS - 1)
+            forward_section(s, w, taps, slope)
 
         return 0
 
@@ -611,7 +607,6 @@
 
     def backward(i, _):
         s = SECTIONS - 1 - i
-        shifted_delta(s, upstream, slope, back)
 
         @pl.when(s == last)
         def _():
@@ -627,21 +622,22 @@
 
         @pl.when(s > last)
         def _():
-            input_grad(s, w, back, upstream)
+            input_grad(s, w, back, slope)
 
         return 0
 
+    store_delta(SECTIONS - 1, upstream[...], slope, back)
     lax.fori_loop(0, SECTIONS - last, backward, 0)
     exchange.to_ring(0, 0)
     exchange.to_ring(0, 1)
     renewal.to_core()
+    gather.finish()
     exchange.across()
     renewal.arrive()
     store = pltpu.make_async_copy(fresh, new_weights, load_sem.at[0])
     store.start()
     exchange.finish(grads)
     renewal.finish()
-    gather.finish()
     store.wait()
 
 
@@ -657,8 +653,8 @@
         out_specs=(vmem, away),
         scratch_shapes=[
             pltpu.VMEM((SECTIONS, ROWS, CHAN), BF16),
-            pltpu.VMEM((SECTIONS, FRAMES, WIDTH + 2, HEIGHT, 3 * CHAN), BF16),
-            pltpu.VMEM((FRAMES, WIDTH + 2, HEIGHT, 3 * CHAN), BF16),
+            pltpu.VMEM((SECTIONS + 1, FRAMES, WIDTH + 2, HEIGHT, 3 * CHAN), BF16),
+            pltpu.VMEM((2, FRAMES, WIDTH + 2, HEIGHT, 3 * CHAN), BF16),
             pltpu.VMEM((SECTIONS, CELLS, CHAN), F32),
             pltpu.VMEM((CELLS, CHAN), F32),
             pltpu.VMEM((SHARD, CHAN), BF16),

time: 67.9 us -> 65.5 us (0.965)
  the two profiles are of different devices: /device:TPU:98 before, /device:TPU:1 now
where the time goes in v7:
time: 65.5 us; the launch traced here: 64.6 us
  Pallas kernels  64 us (98%)
    pallas_call x1, Pallas kernels, window(): pl.pallas_call(window_kernel, out_shape=(shard, jax.ShapeDtypeStruct((2,...  61.7 us
    pallas_call x1, Pallas kernels, finish(): pl.pallas_call(finish_kernel, out_shape=(shard, shard, shard, jax.ShapeDt...  2.26 us

profile of v7, /device:TPU:1, one launch (start us, length us, event | category | flops | bytes accessed | tf_op | source)
XLA Modules:
  0.0 64.6 jit_solution(16890847769292758340)
XLA Ops:
  0.6 61.7 %shard_map.102 = (f32[216,128]{1,0:T(8,128)}, bf16[2,4,2,216,128]{4,3,2,1,0:T(8,128)(2,1)}) custom-call(s32[2,2]{1,0:T(2,128)} %offsets.1, bf16[2,4,384,128]{3,2,1,0:T(8,128)(2,1)} %bitcast.13, bf16[3456,128]{1,0:T(8,128)(2,1)} %bitcast.11, bf16[16,216,128]{2,1,0:T(8,128)(2,1)} %bitcast.12, f32[216,128]{1,0:T(8,128)} %bitcast.14, f32[216,128]{1,0:T(8,128)} %bitcast.16, ...), custom_call_target="tpu_custom_call" | custom-call | tf_op jit(solution)/shard_map/pallas_call | solution.py:649
  62.4 2.3 %shard_map.103 = (f32[216,128]{1,0:T(8,128)}, f32[216,128]{1,0:T(8,128)}, f32[216,128]{1,0:T(8,128)}, bf16[2,4,2,216,128]{4,3,2,1,0:T(8,128)(2,1)}) custom-call(f32[216,128]{1,0:T(8,128)} %get-tuple-element.10.summed, f32[216,128]{1,0:T(8,128)} %bitcast.15, f32[216,128]{1,0:T(8,128)} %bitcast.17, f32[216,128]{1,0:T(8,128)} %bitcast.19, ...), custom_call_target="tpu_custom_call" | custom-call | tf_op jit(solution)/shard_map/pallas_call | solution.py:738

commit v8 on v7

--- a/solution.py
+++ b/solution.py
@@ -288,7 +288,7 @@
         else:
             hops = [
                 (here.at(dy=k), self.mine(s, here.y, 1), self.mine(s, (here.y + 4 - k) % 4, 1))
-                for k in ((1, 3, 2) if mode == RING else (1, 3))
+                for k in ((2, 1, 3) if mode == RING else (1, 3))
             ]
         for n, (device, part, back) in enumerate(hops):
             yield (
@@ -589,7 +589,7 @@
         def _():
             gather.swap(tick)
 
-        s = tick - 1
+        s = tick - 2
 
         @pl.when(s >= 0)
         def _():
@@ -601,7 +601,7 @@
 
         return 0
 
-    lax.fori_loop(0, SECTIONS + 1, forward, 0)
+    lax.fori_loop(0, SECTIONS + 2, forward, 0)
     renewal.to_pair()
     last = 2 * here.z
 

time: 65.5 us -> 64.4 us (0.983)
  Pallas kernels: 64 us -> 63.1 us
    pallas_call x1, Pallas kernels: 61.7 us -> 60.9 us  [window(): pl.pallas_call(window_kernel, out_shape=(shard, jax.ShapeDtypeStruct((2,...]
where the time goes in v8:
time: 64.4 us; the launch traced here: 63.8 us
  Pallas kernels  63.1 us (98%)
    pallas_call x1, Pallas kernels, window(): pl.pallas_call(window_kernel, out_shape=(shard, jax.ShapeDtypeStruct((2,...  60.9 us
    pallas_call x1, Pallas kernels, finish(): pl.pallas_call(finish_kernel, out_shape=(shard, shard, shard, jax.ShapeDt...  2.26 us

profile of v8, /device:TPU:1, one launch (start us, length us, event | category | flops | bytes accessed | tf_op | source)
XLA Modules:
  0.0 63.8 jit_solution(10217363717249466129)
XLA Ops:
  0.6 60.9 %shard_map.102 = (f32[216,128]{1,0:T(8,128)}, bf16[2,4,2,216,128]{4,3,2,1,0:T(8,128)(2,1)}) custom-call(s32[2,2]{1,0:T(2,128)} %offsets.1, bf16[2,4,384,128]{3,2,1,0:T(8,128)(2,1)} %bitcast.13, bf16[3456,128]{1,0:T(8,128)(2,1)} %bitcast.11, bf16[16,216,128]{2,1,0:T(8,128)(2,1)} %bitcast.12, f32[216,128]{1,0:T(8,128)} %bitcast.14, f32[216,128]{1,0:T(8,128)} %bitcast.16, ...), custom_call_target="tpu_custom_call" | custom-call | tf_op jit(solution)/shard_map/pallas_call | solution.py:649
  61.5 2.3 %shard_map.103 = (f32[216,128]{1,0:T(8,128)}, f32[216,128]{1,0:T(8,128)}, f32[216,128]{1,0:T(8,128)}, bf16[2,4,2,216,128]{4,3,2,1,0:T(8,128)(2,1)}) custom-call(f32[216,128]{1,0:T(8,128)} %get-tuple-element.10.summed, f32[216,128]{1,0:T(8,128)} %bitcast.15, f32[216,128]{1,0:T(8,128)} %bitcast.17, f32[216,128]{1,0:T(8,128)} %bitcast.19, ...), custom_call_target="tpu_custom_call" | custom-call | tf_op jit(solution)/shard_map/pallas_call | solution.py:738

commit v9 on v8

--- a/solution.py
+++ b/solution.py
@@ -214,7 +214,7 @@
 MODES = {(1, 0): DIRECT, (3, 0): DIRECT, (2, 0): NEAR, (0, 1): DIRECT, (1, 1): RING, (3, 1): RING, (2, 1): RING}
 ORDER = ((2, 0), (2, 1), (1, 0), (3, 0), (0, 1), (1, 1), (3, 1))
 RELAYS = ((1, 1), (3, 1), (2, 1), (2, 0))
-SENDS = (((1, 1), (2, 1), (3, 1), (2, 0), (0, 1), (1, 0), (3, 0)), ((3, 1), (1, 1), (2, 1), (2, 0), (3, 0), (0, 1), (1, 0)), ((2, 1), (3, 1), (1, 1), (2, 0), (3, 0), (0, 1), (1, 0)), ((1, 1), (2, 1), (3, 1), (2, 0), (1, 0), (3, 0), (0, 1)))
+SENDS = (((2, 1), (3, 1), (1, 1), (2, 0), (0, 1), (3, 0), (1, 0)), ((3, 1), (1, 1), (2, 1), (2, 0), (3, 0), (1, 0), (0, 1)), ((2, 1), (1, 1), (3, 1), (2, 0), (0, 1), (1, 0), (3, 0)), ((1, 1), (3, 1), (2, 1), (2, 0), (1, 0), (3, 0), (0, 1)))
 
 
 class Gather:
@@ -417,8 +417,8 @@
             self.cross_copy(i, 2).start()
 
     def across(self):
-        for i in (1, 0):
-            for lo in range(2):
+        for lo in range(2):
+            for i in (1, 0):
                 self.to_cross(i, lo)
 
     def finish(self, grads):
@@ -611,7 +611,6 @@
         @pl.when(s == last)
         def _():
             exchange.to_ring(1, 0)
-            exchange.to_ring(1, 1)
 
         @pl.when(s < last + 2)
         def _():
@@ -628,6 +627,7 @@
 
     store_delta(SECTIONS - 1, upstream[...], slope, back)
     lax.fori_loop(0, SECTIONS - last, backward, 0)
+    exchange.to_ring(1, 1)
     exchange.to_ring(0, 0)
     exchange.to_ring(0, 1)
     renewal.to_core()

time: 64.4 us -> 64.4 us (level)
  no operation moved by 1% of the time
where the time goes in v9:
time: 64.4 us; the launch traced here: 63.8 us
  Pallas kernels  63.2 us (98%)
    pallas_call x1, Pallas kernels, window(): pl.pallas_call(window_kernel, out_shape=(shard, jax.ShapeDtypeStruct((2,...  60.9 us
    pallas_call x1, Pallas kernels, finish(): pl.pallas_call(finish_kernel, out_shape=(shard, shard, shard, jax.ShapeDt...  2.26 us

profile of v9, /device:TPU:1, one launch (start us, length us, event | category | flops | bytes accessed | tf_op | source)
XLA Modules:
  0.0 63.8 jit_solution(856917039872455991)
XLA Ops:
  0.6 60.9 %shard_map.102 = (f32[216,128]{1,0:T(8,128)}, bf16[2,4,2,216,128]{4,3,2,1,0:T(8,128)(2,1)}) custom-call(s32[2,2]{1,0:T(2,128)} %offsets.1, bf16[2,4,384,128]{3,2,1,0:T(8,128)(2,1)} %bitcast.13, bf16[3456,128]{1,0:T(8,128)(2,1)} %bitcast.11, bf16[16,216,128]{2,1,0:T(8,128)(2,1)} %bitcast.12, f32[216,128]{1,0:T(8,128)} %bitcast.14, f32[216,128]{1,0:T(8,128)} %bitcast.16, ...), custom_call_target="tpu_custom_call" | custom-call | tf_op jit(solution)/shard_map/pallas_call | solution.py:649
  61.5 2.3 %shard_map.103 = (f32[216,128]{1,0:T(8,128)}, f32[216,128]{1,0:T(8,128)}, f32[216,128]{1,0:T(8,128)}, bf16[2,4,2,216,128]{4,3,2,1,0:T(8,128)(2,1)}) custom-call(f32[216,128]{1,0:T(8,128)} %get-tuple-element.10.summed, f32[216,128]{1,0:T(8,128)} %bitcast.15, f32[216,128]{1,0:T(8,128)} %bitcast.17, f32[216,128]{1,0:T(8,128)} %bitcast.19, ...), custom_call_target="tpu_custom_call" | custom-call | tf_op jit(solution)/shard_map/pallas_call | solution.py:738

commit v10 on v8

--- a/solution.py
+++ b/solution.py
@@ -211,10 +211,10 @@
 
 
 DIRECT, PAIR, RING, NEAR = range(4)
-MODES = {(1, 0): DIRECT, (3, 0): DIRECT, (2, 0): NEAR, (0, 1): DIRECT, (1, 1): RING, (3, 1): RING, (2, 1): RING}
+MODES = {(1, 0): PAIR, (3, 0): DIRECT, (2, 0): NEAR, (0, 1): DIRECT, (1, 1): RING, (3, 1): RING, (2, 1): RING}
 ORDER = ((2, 0), (2, 1), (1, 0), (3, 0), (0, 1), (1, 1), (3, 1))
-RELAYS = ((1, 1), (3, 1), (2, 1), (2, 0))
-SENDS = (((1, 1), (2, 1), (3, 1), (2, 0), (0, 1), (1, 0), (3, 0)), ((3, 1), (1, 1), (2, 1), (2, 0), (3, 0), (0, 1), (1, 0)), ((2, 1), (3, 1), (1, 1), (2, 0), (3, 0), (0, 1), (1, 0)), ((1, 1), (2, 1), (3, 1), (2, 0), (1, 0), (3, 0), (0, 1)))
+RELAYS = ((1, 1), (3, 1), (2, 1), (2, 0), (1, 0))
+SENDS = (((1, 1), (2, 1), (3, 1), (2, 0), (1, 0), (0, 1), (3, 0)), ((3, 1), (1, 1), (2, 1), (2, 0), (1, 0), (3, 0), (0, 1)), ((2, 1), (3, 1), (1, 1), (2, 0), (1, 0), (3, 0), (0, 1)), ((1, 1), (2, 1), (3, 1), (2, 0), (1, 0), (3, 0), (0, 1)))
 
 
 class Gather:

time: 64.4 us -> 64.4 us (level)
  no operation moved by 1% of the time
where the time goes in v10:
time: 64.4 us; the launch traced here: 63.8 us
  Pallas kernels  63.1 us (98%)
    pallas_call x1, Pallas kernels, window(): pl.pallas_call(window_kernel, out_shape=(shard, jax.ShapeDtypeStruct((2,...  60.9 us
    pallas_call x1, Pallas kernels, finish(): pl.pallas_call(finish_kernel, out_shape=(shard, shard, shard, jax.ShapeDt...  2.26 us

profile of v10, /device:TPU:1, one launch (start us, length us, event | category | flops | bytes accessed | tf_op | source)
XLA Modules:
  0.0 63.8 jit_solution(13731821411679970621)
XLA Ops:
  0.6 60.9 %shard_map.102 = (f32[216,128]{1,0:T(8,128)}, bf16[2,4,2,216,128]{4,3,2,1,0:T(8,128)(2,1)}) custom-call(s32[2,2]{1,0:T(2,128)} %offsets.1, bf16[2,4,384,128]{3,2,1,0:T(8,128)(2,1)} %bitcast.13, bf16[3456,128]{1,0:T(8,128)(2,1)} %bitcast.11, bf16[16,216,128]{2,1,0:T(8,128)(2,1)} %bitcast.12, f32[216,128]{1,0:T(8,128)} %bitcast.14, f32[216,128]{1,0:T(8,128)} %bitcast.16, ...), custom_call_target="tpu_custom_call" | custom-call | tf_op jit(solution)/shard_map/pallas_call | solution.py:649
  61.5 2.3 %shard_map.103 = (f32[216,128]{1,0:T(8,128)}, f32[216,128]{1,0:T(8,128)}, f32[216,128]{1,0:T(8,128)}, bf16[2,4,2,216,128]{4,3,2,1,0:T(8,128)(2,1)}) custom-call(f32[216,128]{1,0:T(8,128)} %get-tuple-element.10.summed, f32[216,128]{1,0:T(8,128)} %bitcast.15, f32[216,128]{1,0:T(8,128)} %bitcast.17, f32[216,128]{1,0:T(8,128)} %bitcast.19, ...), custom_call_target="tpu_custom_call" | custom-call | tf_op jit(solution)/shard_map/pallas_call | solution.py:738
